TPU v7x, 512 devices: a whole 4x8x8 slice. The times are simulated.
512 devices in a mesh: leaf: 128 (over z, y, core), sep: 4 (over x).
Axes of the slice: x: 4, y: 8, z: 8, core: 2. Of those that a mesh axis runs over, the one named last changes fastest.
Arguments:
- leaf_source: float32 [128, 640, 256], P('leaf', 'sep'), may hold values from -6 to 6
- leaf_inverse: float32 [128, 640, 640], P('leaf', 'sep'), as said below
- leaf_update: float32 [128, 896, 640], P('leaf', None, 'sep'), as said below
- row_lists: int32 [128, 896], P('leaf'), may hold values from 0 to 255
- row_counts: int32 [128, 7], P('leaf'), may hold values from 1 to 128, as said below
- separator_source: float32 [128, 256, 256], P('leaf', 'sep'), may hold values from -6 to 6
- separator_inverse: float32 [128, 256, 256], P('leaf'), as said below
- separator_coupling: float32 [128, 256, 256], P('leaf'), may hold values from -0.1875 to 0.1875
Outputs:
- leaf_solution: float32 [128, 640, 256], P('leaf', 'sep')
- separator_solution: float32 [128, 256, 256], P('leaf', 'sep')
Inputs may be any that keep to these rules, and one draw needn't show every extreme that they name: `leaf_inverse`: each leaf's block is lower triangular, zero above the diagonal, with diagonal entries between 0.6 and 1.4. `separator_inverse`: each block is lower triangular, zero above the diagonal, with diagonal entries between 0.6 and 1.4. `leaf_update`: row r of a leaf's block belongs to the leaf's ancestor of level 1 + r // 128. `row_lists`: entry r names a row of the leaf's ancestor of level 1 + r // 128. `row_counts`: at every level some leaf has 128 live rows.
All inputs are finite; a program needn't handle non-finite values.
Results may differ from a plain program's by a relative error of at most 0.00011.
Values sent between devices are 32-bit elements; how exact they have to be, the bound alone decides.
A program may use at most 64 MiB of HBM per device.

v0:
```python
import jax
import jax.numpy as jnp
from jax import lax
from jax.sharding import PartitionSpec as P

highest = lax.Precision.HIGHEST


def passed_along(x, axis, by):
    peers = lax.axis_size(axis)
    pairs = [(i, i + by) for i in range(peers) if 0 <= i + by < peers]
    return lax.ppermute(x, axis, pairs)


def product(matrix, operand):
    return jnp.dot(matrix, operand, precision=highest, preferred_element_type=jnp.float32)


def product_first(matrix, operand):
    return lax.dot_general(
        matrix,
        operand,
        (((0,), (0,)), ((), ())),
        precision=highest,
        preferred_element_type=jnp.float32,
    )


def tree_pass(payload, offset):
    return passed_along(payload, "leaf", offset)


def sep_rows(payload):
    return lax.all_gather(payload, "sep", axis=0, tiled=True)


def per_device(
    leaf_source,
    leaf_inverse,
    leaf_update,
    row_lists,
    row_counts,
    separator_source,
    separator_inverse,
    separator_coupling,
):
    depth = row_counts.shape[1]
    leaf_index = lax.axis_index("leaf")
    sep_index = lax.axis_index("sep")
    source = leaf_source[0]
    inverse = leaf_inverse[0]
    update = leaf_update[0]
    quarter = separator_source.shape[1]
    full_rows = separator_inverse.shape[1]
    columns = source.shape[1]
    capacity = row_lists.shape[1] // depth
    first_row = sep_index * quarter
    inverse_block = inverse
    leaf_y = product(inverse_block, lax.all_gather(source, "sep", axis=0, tiled=True))
    slot_index = jnp.arange(depth * capacity) % capacity
    limits = jnp.repeat(row_counts[0], capacity)
    live_rows = (slot_index < limits)[:, None]
    update_terms = jnp.where(live_rows, product(update, leaf_y), 0.0)
    targets = row_lists[0].reshape(depth, capacity)
    picker = (jnp.arange(full_rows)[None, :, None] == targets[:, None, :]).astype(jnp.float32)
    densified = jnp.einsum(
        "kwp,kpn->wkn",
        picker,
        update_terms.reshape(depth, capacity, columns),
        precision=highest,
        preferred_element_type=jnp.float32,
    )
    carried = lax.psum_scatter(densified, "sep", scatter_dimension=0, tiled=True)
    own_source = separator_source[0]
    solver_block = separator_inverse[0]
    coupling = separator_coupling[0]
    coupling_rows = lax.dynamic_slice_in_dim(coupling, first_row, quarter, 0)
    solved_down = jnp.zeros((full_rows, columns), jnp.float32)
    for height in range(1, depth + 1):
        upper_slots = carried[:, height - 1 :]
        stride = 2 ** max(height - 2, 0)
        from_left = tree_pass(upper_slots, stride)
        if height == 1:
            from_right = upper_slots
        else:
            from_right = tree_pass(upper_slots, -stride)
        is_owner = leaf_index % 2**height == 2 ** (height - 1)
        carried = carried.at[:, height - 1 :].set(
            jnp.where(is_owner, from_left + from_right, upper_slots)
        )
        residual_full = sep_rows(own_source - carried[:, height - 1])
        solved = product(solver_block, residual_full)
        solved_down = jnp.where(is_owner, solved, solved_down)
        if height < depth:
            carried = carried.at[:, height].add(
                jnp.where(is_owner, product(coupling_rows, solved), 0.0)
            )
    stacked = jnp.zeros(carried.shape, jnp.float32)
    solution_full = jnp.zeros((full_rows, columns), jnp.float32)
    for height in range(depth, 0, -1):
        is_owner = leaf_index % 2**height == 2 ** (height - 1)
        target = solved_down
        if height < depth:
            stride = 2 ** (height - 1)
            upper_slots = stacked[:, height:]
            from_below = tree_pass(upper_slots, stride)
            from_above = tree_pass(upper_slots, -stride)
            right_child = leaf_index // 2**height % 2 == 1
            received = jnp.where(right_child, from_below, from_above)
            stacked = stacked.at[:, height:].set(jnp.where(is_owner, received, upper_slots))
            parent_full = sep_rows(received[:, 0])
            target = solved_down - product_first(coupling, parent_full)
        solution = product_first(solver_block, target)
        solution_full = jnp.where(is_owner, solution, solution_full)
        own_rows = lax.dynamic_slice_in_dim(solution, first_row, quarter, 0)
        stacked = stacked.at[:, height - 1].set(
            jnp.where(is_owner, own_rows, stacked[:, height - 1])
        )
    from_next = tree_pass(stacked, -1)
    ancestors = jnp.where(leaf_index % 2 == 1, stacked, from_next)
    ancestors_full = sep_rows(ancestors)
    picked = jnp.einsum(
        "kwp,wkn->kpn",
        picker,
        ancestors_full,
        precision=highest,
        preferred_element_type=jnp.float32,
    )
    picked = jnp.where(live_rows, picked.reshape(depth * capacity, columns), 0.0)
    leaf_w = leaf_y - product_first(update, picked)
    inverse_block = inverse
    leaf_x = lax.psum_scatter(
        product_first(inverse_block, leaf_w), "sep", scatter_dimension=0, tiled=True
    )
    separator_rows = lax.dynamic_slice_in_dim(solution_full, first_row, quarter, 0)
    return (leaf_x[None], separator_rows[None])


def solution(mesh):
    placed = (
        P("leaf", "sep", None),
        P("leaf", "sep", None),
        P("leaf", None, "sep"),
        P("leaf", None),
        P("leaf", None),
        P("leaf", "sep", None),
        P("leaf", None, None),
        P("leaf", None, None),
    )
    return jax.shard_map(
        per_device,
        mesh=mesh,
        in_specs=placed,
        out_specs=(P("leaf", "sep", None), P("leaf", "sep", None)),
        check_vma=False,
    )
```

profile of v0, /device:TPU:1, one launch (start us, length us, event | category | flops | bytes accessed | tf_op | source)
XLA Modules:
  0.0 518.0 jit_solution(3606953752508697259)
XLA Ops:
  7.2 11.7 %all-gather = f32[1,640,256]{2,1,0:T(8,128)S(1)} all-gather(f32[1,160,256]{2,1,0:T(8,128)} %param.62), channel_id=2, replica_groups=mesh['leaf'=128,'sep'=4] {'sep'}, dimensions={1}, use_global_device_ids=true | all-gather | bytes 819200 | tf_op jit(solution)/shard_map/all_gather | solution.py:59
  19.6 1.6 fusion.8
  23.7 2.0 copy.66
  25.8 42.8 %reduce-scatter.5.cloned.1.call-done = f32[64,7,256]{2,1,0:T(8,128)} async-done(((f32[256,7,256]{2,1,0:T(8,128)}), f32[64,7,256]{2,1,0:T(8,128)}) %reduce-scatter.5.cloned.1.call-update) | async-done | bytes 458768 | tf_op jit(solution)/shard_map/reduce_scatter | solution.py:73
  69.8 3.6 collective-permute-start
  73.4 5.4 %collective-permute-done = f32[64,7,256]{2,0,1:T(8,128)S(1)} collective-permute-done((f32[64,7,256]{2,0,1:T(8,128)S(1)}, f32[64,7,256]{2,0,1:T(8,128)S(1)}, u32[]{:S(2)}, u32[]{:S(2)}) %collective-permute-start) | collective-permute-done | bytes 458784 | tf_op jit(solution)/shard_map/ppermute | solution.py:12
  80.0 9.4 %all_gather.46 = f32[256,256]{1,0:T(8,128)S(1)} all-gather(f32[64,256]{1,0:T(8,128)S(1)} %fusion.94), channel_id=1, replica_groups=mesh['leaf'=128,'sep'=4] {'sep'}, dimensions={0}, use_global_device_ids=true | all-gather | bytes 327680 | tf_op jit(solution)/shard_map/all_gather | solution.py:34
  90.4 7.4 %collective-permute-start.1 = (f32[64,6,256]{2,0,1:T(8,128)S(1)}, f32[64,6,256]{2,0,1:T(8,128)S(1)}, u32[]{:S(2)}, u32[]{:S(2)}) collective-permute-start(f32[64,6,256]{2,0,1:T(8,128)S(1)} %slice.686), channel_id=1, source_target_pairs={{0,4},{4,8},{8,12},{12,16},{16,20},{20,24},{24,28},{28,32},{32,36}... | collective-permute-start | bytes 1179656 | tf_op jit(solution)/shard_map/ppermute | solution.py:12
  97.8 1.9 collective-permute-start.2
  99.8 2.8 collective-permute-done.1
  102.5 4.4 collective-permute-done.2
  107.1 9.4 %all_gather.47 = f32[256,256]{1,0:T(8,128)S(1)} all-gather(f32[64,256]{1,0:T(8,128)S(1)} %fusion.92), channel_id=1, replica_groups=mesh['leaf'=128,'sep'=4] {'sep'}, dimensions={0}, use_global_device_ids=true | all-gather | bytes 327680 | tf_op jit(solution)/shard_map/all_gather | solution.py:34
  117.5 3.7 collective-permute-start.3
  121.2 1.3 collective-permute-start.4
  122.5 4.3 collective-permute-done.3
  126.8 4.4 collective-permute-done.4
  131.3 10.0 %all_gather.48 = f32[256,256]{1,0:T(8,128)S(1)} all-gather(f32[64,256]{1,0:T(8,128)S(1)} %fusion.90), channel_id=1, replica_groups=mesh['leaf'=128,'sep'=4] {'sep'}, dimensions={0}, use_global_device_ids=true | all-gather | bytes 327680 | tf_op jit(solution)/shard_map/all_gather | solution.py:34
  142.3 6.1 %collective-permute-start.5 = (f32[64,4,256]{2,0,1:T(8,128)S(1)}, f32[64,4,256]{2,0,1:T(8,128)S(1)}, u32[]{:S(2)}, u32[]{:S(2)}) collective-permute-start(f32[64,4,256]{2,0,1:T(8,128)S(1)} %slice.692), channel_id=1, source_target_pairs={{0,16},{4,20},{8,24},{12,28},{16,32},{20,36},{24,40},{28,44},{32,4... | collective-permute-start | bytes 786440 | tf_op jit(solution)/shard_map/ppermute | solution.py:12
  148.4 1.3 collective-permute-start.6
  149.7 2.0 collective-permute-done.5
  151.7 5.2 %collective-permute-done.6 = f32[64,4,256]{2,0,1:T(8,128)} collective-permute-done((f32[64,4,256]{2,0,1:T(8,128)S(1)}, f32[64,4,256]{2,0,1:T(8,128)}, u32[]{:S(2)}, u32[]{:S(2)}) %collective-permute-start.6) | collective-permute-done | bytes 262176 | tf_op jit(solution)/shard_map/ppermute | solution.py:12
  158.0 11.6 %all_gather.49 = f32[256,256]{1,0:T(8,128)S(1)} all-gather(f32[64,256]{1,0:T(8,128)S(1)} %fusion.88), channel_id=1, replica_groups=mesh['leaf'=128,'sep'=4] {'sep'}, dimensions={0}, use_global_device_ids=true | all-gather | bytes 327680 | tf_op jit(solution)/shard_map/all_gather | solution.py:34
  170.5 6.1 %collective-permute-start.7 = (f32[64,3,256]{2,0,1:T(8,128)S(1)}, f32[64,3,256]{2,0,1:T(8,128)S(1)}, u32[]{:S(2)}, u32[]{:S(2)}) collective-permute-start(f32[64,3,256]{2,0,1:T(8,128)S(1)} %slice.695), channel_id=1, source_target_pairs={{0,32},{4,36},{8,40},{12,44},{16,48},{20,52},{24,56},{28,60},{32,6... | collective-permute-start | bytes 589832 | tf_op jit(solution)/shard_map/ppermute | solution.py:12
  176.6 1.3 collective-permute-start.8
  177.9 3.4 collective-permute-done.7
  181.3 5.7 %collective-permute-done.8 = f32[64,3,256]{2,0,1:T(8,128)S(1)} collective-permute-done((f32[64,3,256]{2,0,1:T(8,128)S(1)}, f32[64,3,256]{2,0,1:T(8,128)S(1)}, u32[]{:S(2)}, u32[]{:S(2)}) %collective-permute-start.8) | collective-permute-done | bytes 196640 | tf_op jit(solution)/shard_map/ppermute | solution.py:12
  187.1 9.7 %all_gather.50 = f32[256,256]{1,0:T(8,128)S(1)} all-gather(f32[64,256]{1,0:T(8,128)S(1)} %fusion.86), channel_id=1, replica_groups=mesh['leaf'=128,'sep'=4] {'sep'}, dimensions={0}, use_global_device_ids=true | all-gather | bytes 327680 | tf_op jit(solution)/shard_map/all_gather | solution.py:34
  197.8 5.2 %collective-permute-start.9 = (f32[64,2,256]{2,0,1:T(8,128)S(1)}, f32[64,2,256]{2,0,1:T(8,128)S(1)}, u32[]{:S(2)}, u32[]{:S(2)}) collective-permute-start(f32[64,2,256]{2,0,1:T(8,128)S(1)} %slice.698), channel_id=1, source_target_pairs={{0,64},{4,68},{8,72},{12,76},{16,80},{20,84},{24,88},{28,92},{32,9... | collective-permute-start | bytes 393224 | tf_op jit(solution)/shard_map/ppermute | solution.py:12
  203.0 1.3 collective-permute-start.10
  204.9 3.9 collective-permute-done.10
  209.8 9.4 %all_gather.51 = f32[256,256]{1,0:T(8,128)S(1)} all-gather(f32[64,256]{1,0:T(8,128)S(1)} %fusion.85), channel_id=1, replica_groups=mesh['leaf'=128,'sep'=4] {'sep'}, dimensions={0}, use_global_device_ids=true | all-gather | bytes 327680 | tf_op jit(solution)/shard_map/all_gather | solution.py:34
  220.1 8.9 %collective-permute-start.11 = (f32[64,1,256]{2,0,1:T(8,128)S(1)}, f32[64,1,256]{2,0,1:T(8,128)S(1)}, u32[]{:S(2)}, u32[]{:S(2)}) collective-permute-start(f32[64,1,256]{2,0,1:T(8,128)S(1)} %slice_add_fusion), channel_id=1, source_target_pairs={{0,128},{4,132},{8,136},{12,140},{16,144},{20,148},{24,152},{28,15... | collective-permute-start | bytes 196616 | tf_op jit(solution)/shard_map/ppermute | solution.py:12
  229.0 1.3 collective-permute-start.12
  230.3 4.6 collective-permute-done.12
  234.9 9.6 %all_gather.52 = f32[256,256]{1,0:T(8,128)S(1)} all-gather(f32[64,256]{1,0:T(8,128)S(1)} %bitcast_subtract_fusion), channel_id=1, replica_groups=mesh['leaf'=128,'sep'=4] {'sep'}, dimensions={0}, use_global_device_ids=true | all-gather | bytes 327680 | tf_op jit(solution)/shard_map/all_gather | solution.py:34
  245.7 6.4 %collective-permute-start.13 = (f32[64,1,256]{2,0,1:T(8,128)S(1)}, f32[64,1,256]{2,0,1:T(8,128)S(1)}, u32[]{:S(2)}, u32[]{:S(2)}) collective-permute-start(f32[64,1,256]{2,0,1:T(8,128)S(1)} %select_bitcast_fusion), channel_id=1, source_target_pairs={{0,128},{4,132},{8,136},{12,140},{16,144},{20,148},{24,152},{28,15... | collective-permute-start | bytes 196616 | tf_op jit(solution)/shard_map/ppermute | solution.py:12
  253.5 4.5 collective-permute-done.14
  258.1 9.9 %all-gather.1 = f32[256,1,256]{2,1,0:T(1,128)S(1)} all-gather(f32[64,1,256]{2,1,0:T(1,128)S(1)} %copy.70), channel_id=3, replica_groups=mesh['leaf'=128,'sep'=4] {'sep'}, dimensions={0}, use_global_device_ids=true | all-gather | bytes 327680 | tf_op jit(solution)/shard_map/all_gather | solution.py:34
  269.3 1.7 collective-permute-start.15
  270.9 1.3 collective-permute-start.16
  272.9 4.4 collective-permute-done.16
  277.4 10.3 %all-gather.2 = f32[256,1,256]{2,1,0:T(1,128)S(1)} all-gather(f32[64,1,256]{2,1,0:T(1,128)S(1)} %copy.71), channel_id=4, replica_groups=mesh['leaf'=128,'sep'=4] {'sep'}, dimensions={0}, use_global_device_ids=true | all-gather | bytes 327680 | tf_op jit(solution)/shard_map/all_gather | solution.py:34
  289.0 6.4 %collective-permute-start.17 = (f32[64,3,256]{2,0,1:T(8,128)S(1)}, f32[64,3,256]{2,0,1:T(8,128)S(1)}, u32[]{:S(2)}, u32[]{:S(2)}) collective-permute-start(f32[64,3,256]{2,0,1:T(8,128)S(1)} %slice.705), channel_id=1, source_target_pairs={{0,32},{4,36},{8,40},{12,44},{16,48},{20,52},{24,56},{28,60},{32,6... | collective-permute-start | bytes 589832 | tf_op jit(solution)/shard_map/ppermute | solution.py:12
  296.7 3.4 collective-permute-done.17
  300.1 5.7 %collective-permute-done.18 = f32[64,3,256]{2,0,1:T(8,128)S(1)} collective-permute-done((f32[64,3,256]{2,0,1:T(8,128)S(1)}, f32[64,3,256]{2,0,1:T(8,128)S(1)}, u32[]{:S(2)}, u32[]{:S(2)}) %collective-permute-start.18) | collective-permute-done | bytes 196640 | tf_op jit(solution)/shard_map/ppermute | solution.py:12
  306.0 10.1 %all-gather.3 = f32[256,1,256]{2,1,0:T(1,128)S(1)} all-gather(f32[64,1,256]{2,1,0:T(1,128)S(1)} %copy.72), channel_id=5, replica_groups=mesh['leaf'=128,'sep'=4] {'sep'}, dimensions={0}, use_global_device_ids=true | all-gather | bytes 327680 | tf_op jit(solution)/shard_map/all_gather | solution.py:34
  318.0 4.7 collective-permute-start.19
  324.1 3.4 collective-permute-done.19
  327.4 4.3 collective-permute-done.20
  332.0 10.0 %all-gather.4 = f32[256,1,256]{2,1,0:T(1,128)S(1)} all-gather(f32[64,1,256]{2,1,0:T(1,128)S(1)} %copy.73), channel_id=6, replica_groups=mesh['leaf'=128,'sep'=4] {'sep'}, dimensions={0}, use_global_device_ids=true | all-gather | bytes 327680 | tf_op jit(solution)/shard_map/all_gather | solution.py:34
  343.8 7.7 %collective-permute-start.21 = (f32[64,5,256]{2,0,1:T(8,128)S(1)}, f32[64,5,256]{2,0,1:T(8,128)S(1)}, u32[]{:S(2)}, u32[]{:S(2)}) collective-permute-start(f32[64,5,256]{2,0,1:T(8,128)S(1)} %slice.711), channel_id=1, source_target_pairs={{0,8},{4,12},{8,16},{12,20},{16,24},{20,28},{24,32},{28,36},{32,40... | collective-permute-start | bytes 983048 | tf_op jit(solution)/shard_map/ppermute | solution.py:12
  352.9 2.7 collective-permute-done.21
  355.6 3.8 collective-permute-done.22
  359.6 9.6 %all-gather.5 = f32[256,1,256]{2,1,0:T(1,128)S(1)} all-gather(f32[64,1,256]{2,1,0:T(1,128)S(1)} %copy.74), channel_id=7, replica_groups=mesh['leaf'=128,'sep'=4] {'sep'}, dimensions={0}, use_global_device_ids=true | all-gather | bytes 327680 | tf_op jit(solution)/shard_map/all_gather | solution.py:34
  371.2 44.1 %collective-permute-start.23 = (f32[64,6,256]{2,0,1:T(8,128)S(1)}, f32[64,6,256]{2,0,1:T(8,128)S(1)}, u32[]{:S(2)}, u32[]{:S(2)}) collective-permute-start(f32[64,6,256]{2,0,1:T(8,128)S(1)} %slice.714), channel_id=1, source_target_pairs={{0,4},{4,8},{8,12},{12,16},{16,20},{20,24},{24,28},{28,32},{32,36}... | collective-permute-start | bytes 1179656 | tf_op jit(solution)/shard_map/ppermute | solution.py:12
  415.3 1.9 collective-permute-start.24
  417.3 2.7 collective-permute-done.23
  420.0 4.6 collective-permute-done.24
  424.9 9.8 %all-gather.6 = f32[256,1,256]{2,1,0:T(1,128)S(1)} all-gather(f32[64,1,256]{2,1,0:T(1,128)S(1)} %copy.75), channel_id=8, replica_groups=mesh['leaf'=128,'sep'=4] {'sep'}, dimensions={0}, use_global_device_ids=true | all-gather | bytes 327680 | tf_op jit(solution)/shard_map/all_gather | solution.py:34
  435.9 1.9 collective-permute-start.25
  437.8 8.3 %collective-permute-done.25 = f32[64,7,256]{2,0,1:T(8,128)S(1)} collective-permute-done((f32[64,7,256]{2,0,1:T(8,128)S(1)}, f32[64,7,256]{2,0,1:T(8,128)S(1)}, u32[]{:S(2)}, u32[]{:S(2)}) %collective-permute-start.25) | collective-permute-done | bytes 458784 | tf_op jit(solution)/shard_map/ppermute | solution.py:12
  447.4 30.9 %all-gather.9.cloned.1.call-done = f32[256,7,256]{2,0,1:T(8,128)} async-done(((f32[64,7,256]{2,0,1:T(8,128)}), f32[256,7,256]{2,0,1:T(8,128)}) %all-gather.9.cloned.1.call-update) | async-done | bytes 1835024 | tf_op jit(solution)/shard_map/all_gather | solution.py:34
  478.3 2.4 convolution_select_fusion
  485.1 24.5 %reduce-scatter.7.cloned.1.call-done = f32[160,256]{1,0:T(8,128)} async-done(((f32[640,256]{1,0:T(8,128)}), f32[160,256]{1,0:T(8,128)}) %reduce-scatter.7.cloned.1.call-update) | async-done | bytes 163856
  (139 shorter events, 39.1 us)
Async XLA Ops:
  7.2 14.1 %copy-start = (f32[1,896,160]{1,2,0:T(8,128)S(1)}, f32[1,896,160]{1,2,0:T(8,128)}, u32[]{:S(2)}) copy-start(f32[1,896,160]{1,2,0:T(8,128)} %param.64) | copy-start | bytes 1720324
  7.2 61.4 %reduce-scatter.5.cloned.1.call-start = ((), (), s32[]{:S(2)}) async-start(), calls=%async_computation.2 | async-start | bytes 2621440 | tf_op jit(solution)/shard_map/reduce_scatter | solution.py:73
  21.2 1.4 copy-start.10
  22.6 3.1 copy-start.8
  25.7 54.3 %copy-start.3 = (f32[1,64,256]{2,1,0:T(8,128)S(1)}, f32[1,64,256]{2,1,0:T(8,128)}, u32[]{:S(2)}) copy-start(f32[1,64,256]{2,1,0:T(8,128)} %param.67) | copy-start | bytes 196612
  25.7 63.7 %copy-start.1 = (f32[1,256,256]{2,1,0:T(8,128)S(1)}, f32[1,256,256]{2,1,0:T(8,128)}, u32[]{:S(2)}) copy-start(f32[1,256,256]{2,1,0:T(8,128)} %param.68) | copy-start | bytes 786436
  25.7 64.3 %copy-start.2 = (f32[1,256,256]{2,1,0:T(8,128)S(1)}, f32[1,256,256]{2,1,0:T(8,128)}, u32[]{:S(2)}) copy-start(f32[1,256,256]{2,1,0:T(8,128)} %param.69) | copy-start | bytes 786436
  25.7 452.5 %all-gather.9.cloned.1.call-start = ((), (), s32[]{:S(2)}) async-start(), calls=%async_computation.3 | async-start | bytes 2293760 | tf_op jit(solution)/shard_map/all_gather | solution.py:34
  69.8 9.0 %collective-permute-start = (f32[64,7,256]{2,0,1:T(8,128)S(1)}, f32[64,7,256]{2,0,1:T(8,128)S(1)}, u32[]{:S(2)}, u32[]{:S(2)}) collective-permute-start(f32[64,7,256]{2,0,1:T(8,128)S(1)} %copy.67), channel_id=1, source_target_pairs={{0,4},{4,8},{8,12},{12,16},{16,20},{20,24},{24,28},{28,32},{32,36}... | collective-permute-start | bytes 1376264 | tf_op jit(solution)/shard_map/ppermute | solution.py:12
  90.4 12.1 %collective-permute-start.1 = (f32[64,6,256]{2,0,1:T(8,128)S(1)}, f32[64,6,256]{2,0,1:T(8,128)S(1)}, u32[]{:S(2)}, u32[]{:S(2)}) collective-permute-start(f32[64,6,256]{2,0,1:T(8,128)S(1)} %slice.686), channel_id=1, source_target_pairs={{0,4},{4,8},{8,12},{12,16},{16,20},{20,24},{24,28},{28,32},{32,36}... | collective-permute-start | bytes 1179656 | tf_op jit(solution)/shard_map/ppermute | solution.py:12
  97.8 9.1 %collective-permute-start.2 = (f32[64,6,256]{2,0,1:T(8,128)S(1)}, f32[64,6,256]{2,0,1:T(8,128)S(1)}, u32[]{:S(2)}, u32[]{:S(2)}) collective-permute-start(f32[64,6,256]{2,0,1:T(8,128)S(1)} %slice.686), channel_id=1, source_target_pairs={{4,0},{8,4},{12,8},{16,12},{20,16},{24,20},{28,24},{32,28},{36,32}... | collective-permute-start | bytes 1179656 | tf_op jit(solution)/shard_map/ppermute | solution.py:12
  117.5 9.3 %collective-permute-start.3 = (f32[64,5,256]{2,0,1:T(8,128)S(1)}, f32[64,5,256]{2,0,1:T(8,128)S(1)}, u32[]{:S(2)}, u32[]{:S(2)}) collective-permute-start(f32[64,5,256]{2,0,1:T(8,128)S(1)} %slice.689), channel_id=1, source_target_pairs={{0,8},{4,12},{8,16},{12,20},{16,24},{20,28},{24,32},{28,36},{32,40... | collective-permute-start | bytes 983048 | tf_op jit(solution)/shard_map/ppermute | solution.py:12
  121.2 10.0 %collective-permute-start.4 = (f32[64,5,256]{2,0,1:T(8,128)S(1)}, f32[64,5,256]{2,0,1:T(8,128)S(1)}, u32[]{:S(2)}, u32[]{:S(2)}) collective-permute-start(f32[64,5,256]{2,0,1:T(8,128)S(1)} %slice.689), channel_id=1, source_target_pairs={{8,0},{12,4},{16,8},{20,12},{24,16},{28,20},{32,24},{36,28},{40,32... | collective-permute-start | bytes 983048 | tf_op jit(solution)/shard_map/ppermute | solution.py:12
  142.3 9.4 %collective-permute-start.5 = (f32[64,4,256]{2,0,1:T(8,128)S(1)}, f32[64,4,256]{2,0,1:T(8,128)S(1)}, u32[]{:S(2)}, u32[]{:S(2)}) collective-permute-start(f32[64,4,256]{2,0,1:T(8,128)S(1)} %slice.692), channel_id=1, source_target_pairs={{0,16},{4,20},{8,24},{12,28},{16,32},{20,36},{24,40},{28,44},{32,4... | collective-permute-start | bytes 786440 | tf_op jit(solution)/shard_map/ppermute | solution.py:12
  148.4 8.5 %collective-permute-start.6 = (f32[64,4,256]{2,0,1:T(8,128)S(1)}, f32[64,4,256]{2,0,1:T(8,128)}, u32[]{:S(2)}, u32[]{:S(2)}) collective-permute-start(f32[64,4,256]{2,0,1:T(8,128)S(1)} %slice.692), channel_id=1, source_target_pairs={{16,0},{20,4},{24,8},{28,12},{32,16},{36,20},{40,24},{44,28},{48,3... | collective-permute-start | bytes 786440 | tf_op jit(solution)/shard_map/ppermute | solution.py:12
  170.5 10.8 %collective-permute-start.7 = (f32[64,3,256]{2,0,1:T(8,128)S(1)}, f32[64,3,256]{2,0,1:T(8,128)S(1)}, u32[]{:S(2)}, u32[]{:S(2)}) collective-permute-start(f32[64,3,256]{2,0,1:T(8,128)S(1)} %slice.695), channel_id=1, source_target_pairs={{0,32},{4,36},{8,40},{12,44},{16,48},{20,52},{24,56},{28,60},{32,6... | collective-permute-start | bytes 589832 | tf_op jit(solution)/shard_map/ppermute | solution.py:12
  176.6 10.4 %collective-permute-start.8 = (f32[64,3,256]{2,0,1:T(8,128)S(1)}, f32[64,3,256]{2,0,1:T(8,128)S(1)}, u32[]{:S(2)}, u32[]{:S(2)}) collective-permute-start(f32[64,3,256]{2,0,1:T(8,128)S(1)} %slice.695), channel_id=1, source_target_pairs={{32,0},{36,4},{40,8},{44,12},{48,16},{52,20},{56,24},{60,28},{64,3... | collective-permute-start | bytes 589832 | tf_op jit(solution)/shard_map/ppermute | solution.py:12
  197.8 7.1 %collective-permute-start.9 = (f32[64,2,256]{2,0,1:T(8,128)S(1)}, f32[64,2,256]{2,0,1:T(8,128)S(1)}, u32[]{:S(2)}, u32[]{:S(2)}) collective-permute-start(f32[64,2,256]{2,0,1:T(8,128)S(1)} %slice.698), channel_id=1, source_target_pairs={{0,64},{4,68},{8,72},{12,76},{16,80},{20,84},{24,88},{28,92},{32,9... | collective-permute-start | bytes 393224 | tf_op jit(solution)/shard_map/ppermute | solution.py:12
  203.0 5.8 %collective-permute-start.10 = (f32[64,2,256]{2,0,1:T(8,128)S(1)}, f32[64,2,256]{2,0,1:T(8,128)}, u32[]{:S(2)}, u32[]{:S(2)}) collective-permute-start(f32[64,2,256]{2,0,1:T(8,128)S(1)} %slice.698), channel_id=1, source_target_pairs={{64,0},{68,4},{72,8},{76,12},{80,16},{84,20},{88,24},{92,28},{96,3... | collective-permute-start | bytes 393224 | tf_op jit(solution)/shard_map/ppermute | solution.py:12
  220.1 10.2 %collective-permute-start.11 = (f32[64,1,256]{2,0,1:T(8,128)S(1)}, f32[64,1,256]{2,0,1:T(8,128)S(1)}, u32[]{:S(2)}, u32[]{:S(2)}) collective-permute-start(f32[64,1,256]{2,0,1:T(8,128)S(1)} %slice_add_fusion), channel_id=1, source_target_pairs={{0,128},{4,132},{8,136},{12,140},{16,144},{20,148},{24,152},{28,15... | collective-permute-start | bytes 196616 | tf_op jit(solution)/shard_map/ppermute | solution.py:12
  229.0 5.9 %collective-permute-start.12 = (f32[64,1,256]{2,0,1:T(8,128)S(1)}, f32[64,1,256]{2,0,1:T(8,128)S(1)}, u32[]{:S(2)}, u32[]{:S(2)}) collective-permute-start(f32[64,1,256]{2,0,1:T(8,128)S(1)} %slice_add_fusion), channel_id=1, source_target_pairs={{128,0},{132,4},{136,8},{140,12},{144,16},{148,20},{152,24},{156,2... | collective-permute-start | bytes 196616 | tf_op jit(solution)/shard_map/ppermute | solution.py:12
  245.7 7.8 %collective-permute-start.13 = (f32[64,1,256]{2,0,1:T(8,128)S(1)}, f32[64,1,256]{2,0,1:T(8,128)S(1)}, u32[]{:S(2)}, u32[]{:S(2)}) collective-permute-start(f32[64,1,256]{2,0,1:T(8,128)S(1)} %select_bitcast_fusion), channel_id=1, source_target_pairs={{0,128},{4,132},{8,136},{12,140},{16,144},{20,148},{24,152},{28,15... | collective-permute-start | bytes 196616 | tf_op jit(solution)/shard_map/ppermute | solution.py:12
  252.1 5.9 %collective-permute-start.14 = (f32[64,1,256]{2,0,1:T(8,128)S(1)}, f32[64,1,256]{2,0,1:T(8,128)S(1)}, u32[]{:S(2)}, u32[]{:S(2)}) collective-permute-start(f32[64,1,256]{2,0,1:T(8,128)S(1)} %select_bitcast_fusion), channel_id=1, source_target_pairs={{128,0},{132,4},{136,8},{140,12},{144,16},{148,20},{152,24},{156,2... | collective-permute-start | bytes 196616 | tf_op jit(solution)/shard_map/ppermute | solution.py:12
  269.3 3.6 collective-permute-start.15
  270.9 6.3 %collective-permute-start.16 = (f32[64,2,256]{2,0,1:T(8,128)S(1)}, f32[64,2,256]{2,0,1:T(8,128)S(1)}, u32[]{:S(2)}, u32[]{:S(2)}) collective-permute-start(f32[64,2,256]{2,0,1:T(8,128)S(1)} %slice.702), channel_id=1, source_target_pairs={{64,0},{68,4},{72,8},{76,12},{80,16},{84,20},{88,24},{92,28},{96,3... | collective-permute-start | bytes 393224 | tf_op jit(solution)/shard_map/ppermute | solution.py:12
  289.0 11.1 %collective-permute-start.17 = (f32[64,3,256]{2,0,1:T(8,128)S(1)}, f32[64,3,256]{2,0,1:T(8,128)S(1)}, u32[]{:S(2)}, u32[]{:S(2)}) collective-permute-start(f32[64,3,256]{2,0,1:T(8,128)S(1)} %slice.705), channel_id=1, source_target_pairs={{0,32},{4,36},{8,40},{12,44},{16,48},{20,52},{24,56},{28,60},{32,6... | collective-permute-start | bytes 589832 | tf_op jit(solution)/shard_map/ppermute | solution.py:12
  295.4 10.4 %collective-permute-start.18 = (f32[64,3,256]{2,0,1:T(8,128)S(1)}, f32[64,3,256]{2,0,1:T(8,128)S(1)}, u32[]{:S(2)}, u32[]{:S(2)}) collective-permute-start(f32[64,3,256]{2,0,1:T(8,128)S(1)} %slice.705), channel_id=1, source_target_pairs={{32,0},{36,4},{40,8},{44,12},{48,16},{52,20},{56,24},{60,28},{64,3... | collective-permute-start | bytes 589832 | tf_op jit(solution)/shard_map/ppermute | solution.py:12
  318.0 9.4 %collective-permute-start.19 = (f32[64,4,256]{2,0,1:T(8,128)S(1)}, f32[64,4,256]{2,0,1:T(8,128)S(1)}, u32[]{:S(2)}, u32[]{:S(2)}) collective-permute-start(f32[64,4,256]{2,0,1:T(8,128)S(1)} %slice.708), channel_id=1, source_target_pairs={{0,16},{4,20},{8,24},{12,28},{16,32},{20,36},{24,40},{28,44},{32,4... | collective-permute-start | bytes 786440 | tf_op jit(solution)/shard_map/ppermute | solution.py:12
  322.7 9.0 %collective-permute-start.20 = (f32[64,4,256]{2,0,1:T(8,128)S(1)}, f32[64,4,256]{2,0,1:T(8,128)S(1)}, u32[]{:S(2)}, u32[]{:S(2)}) collective-permute-start(f32[64,4,256]{2,0,1:T(8,128)S(1)} %slice.708), channel_id=1, source_target_pairs={{16,0},{20,4},{24,8},{28,12},{32,16},{36,20},{40,24},{44,28},{48,3... | collective-permute-start | bytes 786440 | tf_op jit(solution)/shard_map/ppermute | solution.py:12
  343.8 11.7 %collective-permute-start.21 = (f32[64,5,256]{2,0,1:T(8,128)S(1)}, f32[64,5,256]{2,0,1:T(8,128)S(1)}, u32[]{:S(2)}, u32[]{:S(2)}) collective-permute-start(f32[64,5,256]{2,0,1:T(8,128)S(1)} %slice.711), channel_id=1, source_target_pairs={{0,8},{4,12},{8,16},{12,20},{16,24},{20,28},{24,32},{28,36},{32,40... | collective-permute-start | bytes 983048 | tf_op jit(solution)/shard_map/ppermute | solution.py:12
  351.6 7.8 %collective-permute-start.22 = (f32[64,5,256]{2,0,1:T(8,128)S(1)}, f32[64,5,256]{2,0,1:T(8,128)S(1)}, u32[]{:S(2)}, u32[]{:S(2)}) collective-permute-start(f32[64,5,256]{2,0,1:T(8,128)S(1)} %slice.711), channel_id=1, source_target_pairs={{8,0},{12,4},{16,8},{20,12},{24,16},{28,20},{32,24},{36,28},{40,32... | collective-permute-start | bytes 983048 | tf_op jit(solution)/shard_map/ppermute | solution.py:12
  371.2 48.8 %collective-permute-start.23 = (f32[64,6,256]{2,0,1:T(8,128)S(1)}, f32[64,6,256]{2,0,1:T(8,128)S(1)}, u32[]{:S(2)}, u32[]{:S(2)}) collective-permute-start(f32[64,6,256]{2,0,1:T(8,128)S(1)} %slice.714), channel_id=1, source_target_pairs={{0,4},{4,8},{8,12},{12,16},{16,20},{20,24},{24,28},{28,32},{32,36}... | collective-permute-start | bytes 1179656 | tf_op jit(solution)/shard_map/ppermute | solution.py:12
  415.3 9.3 %collective-permute-start.24 = (f32[64,6,256]{2,0,1:T(8,128)S(1)}, f32[64,6,256]{2,0,1:T(8,128)S(1)}, u32[]{:S(2)}, u32[]{:S(2)}) collective-permute-start(f32[64,6,256]{2,0,1:T(8,128)S(1)} %slice.714), channel_id=1, source_target_pairs={{4,0},{8,4},{12,8},{16,12},{20,16},{24,20},{28,24},{32,28},{36,32}... | collective-permute-start | bytes 1179656 | tf_op jit(solution)/shard_map/ppermute | solution.py:12
  434.6 12.6 %copy-start.11 = (s32[1,7]{1,0:T(1,128)S(1)}, s32[1,7]{1,0:T(1,128)}, u32[]{:S(2)}) copy-start(s32[1,7]{1,0:T(1,128)} %param.66) | copy-start | bytes 88
  434.6 43.6 %copy-start.9 = (s32[896]{0:T(1024)S(1)}, s32[896]{0:T(1024)}, u32[]{:S(2)}) copy-start(s32[896]{0:T(1024)} %copy-done.8) | copy-start | bytes 10756
  435.9 10.2 %collective-permute-start.25 = (f32[64,7,256]{2,0,1:T(8,128)S(1)}, f32[64,7,256]{2,0,1:T(8,128)S(1)}, u32[]{:S(2)}, u32[]{:S(2)}) collective-permute-start(f32[64,7,256]{2,0,1:T(8,128)S(1)} %get-tuple-element.328), channel_id=1, source_target_pairs={{4,0},{8,4},{12,8},{16,12},{20,16},{24,20},{28,24},{32,28},{36,32}... | collective-permute-start | bytes 1376264 | tf_op jit(solution)/shard_map/ppermute | solution.py:12
  447.0 62.6 %reduce-scatter.7.cloned.1.call-start = ((), (), s32[]{:S(2)}) async-start(), calls=%async_computation.4 | async-start | bytes 819200
  447.4 34.1 %copy-start.4 = (f32[1,160,640]{2,1,0:T(8,128)S(1)}, f32[1,160,640]{2,1,0:T(8,128)}, u32[]{:S(2)}) copy-start(f32[1,160,640]{2,1,0:T(8,128)} %param.63) | copy-start | bytes 1228804
  482.3 1.5 copy-start.5
  482.3 1.6 copy-start.6
  482.3 1.7 copy-start.7
Sparse Core Ops, SparseCore 0:
  25.8 42.6 reduce-scatter.4
  447.1 31.1 all-gather.8
  483.6 25.9 reduce-scatter.6
where the time goes:
time: 519 us; the launch traced here: 518 us
  waiting for transfers between devices  193 us (37%)
  blocking collectives  140 us (27%)
  starting transfers between devices  131 us (25%)
  matrix products  21.9 us (4%)
  between operations  15 us (3%)
  local copies, waits for them, and re-layouts  8.57 us (2%)
  other arithmetic  7.86 us (2%)
    ppermute x26, starting transfers between devices, passed_along(): return lax.ppermute(x, axis, pairs)  131 us
    all_gather x13, blocking collectives, sep_rows(): return lax.all_gather(payload, 'sep', axis=0, tiled=True)  129 us
    ppermute x26, waiting for transfers between devices, passed_along(): return lax.ppermute(x, axis, pairs)  95.2 us
    reduce_scatter x1, waiting for transfers between devices, per_device(): lax.psum_scatter(densified, 'sep', scatter_dimension=0, tiled=True)  42.8 us
    all_gather x1, waiting for transfers between devices, sep_rows(): return lax.all_gather(payload, 'sep', axis=0, tiled=True)  30.9 us
    unnamed x4, waiting for transfers between devices  24.6 us
    all_gather x1, blocking collectives, per_device(): lax.all_gather(source, 'sep', axis=0, tiled=True)  11.7 us
  transfers between devices with their start and end apart: 29, of which 27 were waited for; matrix products, arithmetic and copies ran while one was open for 0% of the time, Pallas kernels for 0%

commit v1 on v0

v1 whole, which is shorter than its diff:
```python
import functools

import jax
import jax.numpy as jnp
from jax import lax
from jax.experimental import pallas as pl
from jax.experimental.pallas import tpu as pltpu
from jax.sharding import PartitionSpec as P

MESH = pl.DeviceIdType.MESH
F32 = jnp.float32
BF16 = jnp.bfloat16


def split(x):
    high = x.astype(BF16)
    return high, (x - high.astype(F32)).astype(BF16)


def mm(a, b, ca=1, cb=0):
    return lax.dot_general(a, b, (((ca,), (cb,)), ((), ())), preferred_element_type=F32)


def mm3(a, b, ca=1, cb=0):
    ah, al = split(a)
    bh, bl = split(b)
    return mm(ah, bh, ca, cb) + (mm(al, bh, ca, cb) + mm(ah, bl, ca, cb))


def stacked(matrix):
    high, low = split(matrix)
    return jnp.concatenate([high, high, low], axis=0)


def chain(rows, stack):
    high, low = split(rows)
    return mm(jnp.concatenate([high, low, high], axis=1), stack)


def level_of(index, depth):
    level = jnp.int32(1)
    half = jnp.int32(1)
    for k in range(1, depth + 1):
        hit = (lax.rem(index, 2**k) == 0).astype(jnp.int32)
        level = level + hit
        half = half + hit * 2 ** (k - 1)
    return level, half


def kernel(
    depth,
    counts,
    src,
    inv,
    upd,
    lists,
    ssrc,
    sinv,
    cpl,
    out,
    sol,
    S,
    sp,
    ssb,
    MT3,
    M3,
    N3,
    pick,
    yT,
    updh,
    updl,
    TT,
    rsb,
    D,
    up,
    uo,
    R,
    U,
    V,
    dn,
    pkb,
    XB,
    fb,
    xp,
    xob,
    agS,
    agR,
    ssS,
    ssR,
    rsS,
    rsR,
    eS,
    pS,
    upR,
    dS,
    dnR,
    pkS,
    pkR,
    fS,
    fR,
    xS,
    xR,
):
    l = lax.axis_index("leaf")
    q = lax.axis_index("sep")
    nsep = 4
    rows = src.shape[0]
    cols = ssrc.shape[0]
    cap = lists.shape[1] // depth
    lam, half = level_of(l, depth)
    even = lax.rem(l, 2) == 0
    odd = lax.rem(l, 2) == 1
    lam_pair, _ = level_of(l - 1, depth)
    low_half = lax.div(half, 2)
    right = (lax.rem(l, 4 * half) >= 2 * half).astype(jnp.int32)
    parent = l + half - 2 * half * right
    is_owner = l > 0
    has_parent = lam < depth
    even_owner = jnp.logical_and(even, is_owner)
    pair = l + 1 - 2 * lax.rem(l, 2)

    def at_sep(d):
        return (l, lax.rem(q + d, nsep))

    def hello(device):
        pl.semaphore_signal(barrier, inc=1, device_id=device, device_id_type=MESH)

    def rcopy(a, b, ss, rs, device):
        return pltpu.make_async_remote_copy(
            src_ref=a, dst_ref=b, send_sem=ss, recv_sem=rs, device_id=device, device_id_type=MESH
        )

    barrier = pltpu.get_barrier_semaphore()
    for d in range(1, nsep):
        hello(at_sep(d))
    hello((pair, q))

    @pl.when(has_parent)
    def _():
        hello((parent, q))

    @pl.when(even_owner)
    def _():
        hello((l - low_half, q))
        hello((l + low_half, q))

    own = pl.ds(pl.multiple_of(q * rows, 8), rows)
    mine = pl.ds(pl.multiple_of(q * cols, 8), cols)
    S[own, :] = src[...]
    for j in range(1, nsep):

        @pl.when(j > q)
        def _():
            S[j * rows : (j + 1) * rows, :] = jnp.zeros((rows, S.shape[1]), F32)

    sp[...] = jnp.zeros_like(sp)
    sp[:, :cols] = ssrc[...].T
    ssb[q] = sp[mine, :]

    peers = 4 + has_parent.astype(jnp.int32) + 2 * even_owner.astype(jnp.int32)
    pl.semaphore_wait(barrier, peers)

    def ag(d):
        return rcopy(S.at[own, :], S.at[own, :], agS.at[d], agR.at[d], at_sep(d))

    for d in (2, 1, 3):

        @pl.when(q + d < nsep)
        def _():
            ag(d).start()

    def ssx(d):
        to = lax.rem(q + d, nsep)
        return rcopy(
            sp.at[pl.ds(pl.multiple_of(to * cols, 8), cols), :],
            ssb.at[q],
            ssS.at[d],
            ssR.at[d],
            at_sep(d),
        )

    for d in range(1, nsep):
        ssx(d).start()

    wi = lax.broadcasted_iota(jnp.int32, (pick.shape[1], cap), 0)
    pi = lax.broadcasted_iota(jnp.int32, (pick.shape[1], cap), 1)
    for j in range(depth):
        hit = jnp.logical_and(wi == lists[0:1, j * cap : (j + 1) * cap], pi < counts[0, j])
        pick[j] = jnp.where(hit, 1.0, 0.0).astype(BF16)
    uh, ul = split(upd[...])
    updh[...] = uh
    updl[...] = ul
    M = mm3(cpl[...], sinv[...])
    M3[...] = stacked(M)
    MT3[...] = stacked(M.T)
    N3[...] = stacked(mm3(sinv[...], sinv[...], 0, 0))

    for d in range(1, nsep):

        @pl.when(q - d >= 0)
        def _():
            ag(d).wait_recv()

    yT[...] = mm3(inv[...], S[...]).T

    def rs(j, d):
        to = lax.rem(q + d, nsep)
        return rcopy(
            TT.at[j, pl.ds(pl.multiple_of(to * cols, 8), cols), :],
            rsb.at[j, d],
            rsS.at[j, d],
            rsR.at[j, d],
            at_sep(d),
        )

    yh, yl = split(yT[...])
    for j in range(depth):
        bh = updh[j * cap : (j + 1) * cap, :]
        bl = updl[j * cap : (j + 1) * cap, :]
        TT[j] = mm(yh, bh, 1, 1) + (mm(yl, bh, 1, 1) + mm(yh, bl, 1, 1))
        for d in (2, 1, 3):
            rs(j, d).start()

    for d in range(1, nsep):
        ssx(d).wait_recv()
    sT = jnp.concatenate([ssb[i][:, :cols] for i in range(nsep)], axis=1)

    def to_pair(j):
        return rcopy(D.at[j], up.at[0, j], eS.at[j], upR.at[0, j], (pair, q))

    def to_parent(j):
        return rcopy(uo.at[j], up.at[right, j], pS.at[j], upR.at[right, j], (parent, q))

    def wait_up(side, j):
        rcopy(D.at[0], up.at[side, j], eS.at[0], upR.at[side, j], (pair, q)).wait_recv()

    for j in range(1, depth + 1):
        for d in range(1, nsep):
            rs(j - 1, d).wait_recv()
        t = (TT[j - 1, mine, :] + rsb[j - 1, 1]) + (rsb[j - 1, 2] + rsb[j - 1, 3])
        th, tl = split(t)
        Dj = mm(th, pick[j - 1], 1, 1) + mm(tl, pick[j - 1], 1, 1)

        @pl.when(even)
        def _():
            D[j] = Dj
            to_pair(j).start()

        @pl.when(odd)
        def _():
            wait_up(0, j)
            total = up[0, j] + Dj
            if j == 1:
                R[...] = sT - total
                U[...] = chain(R[...], MT3[...])
            else:
                uo[j] = total + U[...] if j == 2 else total
                to_parent(j).start()

    @pl.when(even_owner)
    def _():
        wait_up(0, lam)
        wait_up(1, lam)
        R[...] = sT - (up[0, lam] + up[1, lam])

        @pl.when(has_parent)
        def _():
            U[...] = chain(R[...], MT3[...])

        for i in range(1, depth - 1):
            j = lam + i

            @pl.when(j <= depth)
            def _():
                wait_up(0, j)
                wait_up(1, j)
                total = up[0, j] + up[1, j]
                uo[j] = total + U[...] if i == 1 else total
                to_parent(j).start()

    @pl.when(is_owner)
    def _():
        V[...] = chain(R[...], N3[...])

    def to_child(j, side):
        device = (l - low_half + half * side, q)
        return rcopy(dn.at[j], dn.at[j], dS.at[side, j], dnR.at[j], device)

    def down_pair(j):
        return rcopy(dn.at[j], dn.at[j], dS.at[0, j], dnR.at[j], (pair, q))

    def forward(j):
        @pl.when(even_owner)
        def _():
            to_child(j, 0).start()
            to_child(j, 1).start()

        @pl.when(jnp.logical_and(odd, j < lam_pair))
        def _():
            down_pair(j).start()

    def pk(j, d):
        place = pkb.at[mine, (j - 1) * cap : j * cap]
        return rcopy(place, place, pkS.at[j, d], pkR.at[j, d], at_sep(d))

    for j in range(depth, 0, -1):

        @pl.when(j != lam)
        def _():
            down_pair(j).wait_recv()

        if j == depth:

            @pl.when(lam == depth)
            def _():
                dn[j] = V[...]
                forward(j)

        if j > 1:

            @pl.when(j == lam + 1)
            def _():
                dn[j - 1] = V[...] - chain(dn[j], M3[...])
                forward(j - 1)

        @pl.when(j > lam)
        def _():
            forward(j)

        xh, xl = split(dn[j])
        pkb[mine, (j - 1) * cap : j * cap] = mm(xh, pick[j - 1]) + mm(xl, pick[j - 1])
        for d in (2, 1, 3):
            pk(j, d).start()

    def xo(d):
        to = lax.rem(q + d, nsep)
        return rcopy(
            xp.at[pl.ds(pl.multiple_of(to * cols, 8), cols), :],
            xob.at[q],
            xS.at[d],
            xR.at[d],
            at_sep(d),
        )

    xp[...] = jnp.zeros_like(xp)

    @pl.when(is_owner)
    def _():
        xp[:, :cols] = dn[lam].T

    xob[q] = xp[mine, :]
    for d in range(1, nsep):
        xo(d).start()

    for j in range(depth, 0, -1):
        for d in range(1, nsep):
            pk(j, d).wait_recv()
    ph, pw = split(pkb[...])
    wT = yT[...] - (mm(ph, updh[...]) + (mm(pw, updh[...]) + mm(ph, updl[...])))
    XB[...] = mm3(inv[...], wT.T, 0, 0)

    def fin(d):
        to = q - d
        return rcopy(
            XB.at[pl.ds(pl.multiple_of(to * rows, 8), rows), :],
            fb.at[d],
            fS.at[d],
            fR.at[d],
            (l, to),
        )

    for d in (2, 1, 3):

        @pl.when(q - d >= 0)
        def _():
            fin(d).start()

    for d in range(1, nsep):
        xo(d).wait_recv()
    sol[...] = jnp.concatenate([xob[i][:, :cols] for i in range(nsep)], axis=1)
    out[...] = XB[own, :]
    for d in range(1, nsep):

        @pl.when(q + d < nsep)
        def _():
            rcopy(XB.at[own, :], fb.at[d], fS.at[d], fR.at[d], at_sep(d)).wait_recv()
            out[...] += fb[d]

    for d in range(1, nsep):

        @pl.when(q + d < nsep)
        def _():
            ag(d).wait_send()

        @pl.when(q - d >= 0)
        def _():
            fin(d).wait_send()

        ssx(d).wait_send()
        xo(d).wait_send()
        for j in range(1, depth + 1):
            rs(j - 1, d).wait_send()
            pk(j, d).wait_send()
    for j in range(1, depth + 1):

        @pl.when(even)
        def _():
            to_pair(j).wait_send()

        @pl.when(jnp.logical_and(is_owner, j > lam))
        def _():
            to_parent(j).wait_send()

        @pl.when(jnp.logical_and(even_owner, j >= lam))
        def _():
            to_child(j, 0).wait_send()
            to_child(j, 1).wait_send()

        @pl.when(jnp.logical_and(odd, j < lam_pair))
        def _():
            down_pair(j).wait_send()


def per_device(src, inv, upd, lists, counts, ssrc, sinv, cpl):
    depth = counts.shape[1]
    rows, n = src.shape[1:]
    order = inv.shape[2]
    urows = upd.shape[1]
    cols = ssrc.shape[1]
    w = sinv.shape[1]
    cap = urows // depth
    nsep = 4
    slots = depth + 1
    dma = pltpu.SemaphoreType.DMA
    vm = pl.BlockSpec(memory_space=pltpu.VMEM)
    out, sol = pl.pallas_call(
        functools.partial(kernel, depth),
        out_shape=(
            jax.ShapeDtypeStruct((rows, n), F32),
            jax.ShapeDtypeStruct((cols, n), F32),
        ),
        in_specs=[pl.BlockSpec(memory_space=pltpu.SMEM)] + [vm] * 7,
        out_specs=(vm, vm),
        scratch_shapes=[
            pltpu.VMEM((order, n), F32),
            pltpu.VMEM((n, 128), F32),
            pltpu.VMEM((nsep, cols, 128), F32),
            pltpu.VMEM((3 * w, w), BF16),
            pltpu.VMEM((3 * w, w), BF16),
            pltpu.VMEM((3 * w, w), BF16),
            pltpu.VMEM((depth, w, cap), BF16),
            pltpu.VMEM((n, rows), F32),
            pltpu.VMEM((urows, rows), BF16),
            pltpu.VMEM((urows, rows), BF16),
            pltpu.VMEM((depth, n, cap), F32),
            pltpu.VMEM((depth, nsep, cols, cap), F32),
            pltpu.VMEM((slots, cols, w), F32),
            pltpu.VMEM((2, slots, cols, w), F32),
            pltpu.VMEM((slots, cols, w), F32),
            pltpu.VMEM((cols, w), F32),
            pltpu.VMEM((cols, w), F32),
            pltpu.VMEM((cols, w), F32),
            pltpu.VMEM((slots, cols, w), F32),
            pltpu.VMEM((n, urows), F32),
            pltpu.VMEM((order, n), F32),
            pltpu.VMEM((nsep, rows, n), F32),
            pltpu.VMEM((n, 128), F32),
            pltpu.VMEM((nsep, cols, 128), F32),
            dma((nsep,)),
            dma((nsep,)),
            dma((nsep,)),
            dma((nsep,)),
            dma((depth, nsep)),
            dma((depth, nsep)),
            dma((slots,)),
            dma((slots,)),
            dma((2, slots)),
            dma((2, slots)),
            dma((slots,)),
            dma((slots, nsep)),
            dma((slots, nsep)),
            dma((nsep,)),
            dma((nsep,)),
            dma((nsep,)),
            dma((nsep,)),
        ],
        compiler_params=pltpu.CompilerParams(
            collective_id=0, has_side_effects=True, vmem_limit_bytes=48 * 2**20
        ),
    )(counts, src[0], inv[0], upd[0], lists, ssrc[0], sinv[0], cpl[0])
    return out[None], sol[None]


def solution(mesh):
    placed = (
        P("leaf", "sep", None),
        P("leaf", "sep", None),
        P("leaf", None, "sep"),
        P("leaf", None),
        P("leaf", None),
        P("leaf", "sep", None),
        P("leaf", None, None),
        P("leaf", None, None),
    )
    return jax.shard_map(
        per_device,
        mesh=mesh,
        in_specs=placed,
        out_specs=(P("leaf", "sep", None), P("leaf", "sep", None)),
        check_vma=False,
    )
```

time: 519 us -> 117 us (0.23)
  waiting for transfers between devices: 193 us -> 0 us
  blocking collectives: 140 us -> 0 us
  starting transfers between devices: 131 us -> 0 us
  Pallas kernels: 0 us -> 113 us
  matrix products: 21.9 us -> 0 us
  between operations: 15 us -> 0.75 us
  other arithmetic: 7.86 us -> 0 us
  local copies, waits for them, and re-layouts: 8.57 us -> 3.35 us
    all_gather x14 -> x0, blocking collectives: 140 us -> none  [the longest x13 129 us: sep_rows(): return lax.all_gather(payload, 'sep', axis=0, tiled=True)]
    ppermute x26 -> x0, starting transfers between devices: 131 us -> none  [passed_along(): return lax.ppermute(x, axis, pairs)]
    pallas_call x0 -> x1, Pallas kernels: none -> 113 us  [per_device(): pl.pallas_call(functools.partial(kernel, depth), out_shape=(jax.ShapeDtyp...]
    ppermute x26 -> x0, waiting for transfers between devices: 95.2 us -> none  [passed_along(): return lax.ppermute(x, axis, pairs)]
    reduce_scatter x1 -> x0, waiting for transfers between devices: 42.8 us -> none  [per_device(): lax.psum_scatter(densified, 'sep', scatter_dimension=0, tiled=True)]
    all_gather x1 -> x0, waiting for transfers between devices: 30.9 us -> none  [sep_rows(): return lax.all_gather(payload, 'sep', axis=0, tiled=True)]
    unnamed x4 -> x0, waiting for transfers between devices: 24.6 us -> none
    dot_general x32 -> x0, matrix products: 21.9 us -> none  [the longest x15 9.33 us: product_first(): lax.dot_general(matrix, operand, (((0,), (0,)), ((), ())), precision=high...]
  transfers between devices with their start and end apart: 29 -> 0, of which waited for: 27 -> 0; matrix products, arithmetic and copies ran while one was open for 0% -> 0% of each run, Pallas kernels for 0% -> 0%
where the time goes in v1:
time: 117 us
  Pallas kernels  113 us (97%)
  local copies, waits for them, and re-layouts  3.35 us (3%)
    pallas_call x1, Pallas kernels, per_device(): pl.pallas_call(functools.partial(kernel, depth), out_shape=(jax.ShapeDtyp...  113 us
    unnamed x17, local copies, waits for them, and re-layouts  3.35 us

profile of v1, /device:TPU:1, one launch (start us, length us, event | category | flops | bytes accessed | tf_op | source)
XLA Modules:
  0.0 117.2 jit_solution(6634820751214327497)
XLA Ops:
  0.6 0.0 copy-start
  0.6 0.0 copy-start.1
  0.7 0.0 copy-start.2
  0.7 0.0 copy-start.3
  0.7 0.0 copy-start.4
  0.7 0.0 copy-start.5
  0.7 1.4 %copy.10 = f32[1,896,160]{2,1,0:T(8,128)S(1)} copy(f32[1,896,160]{1,2,0:T(8,128)} %param.10) | data formatting | bytes 1146880 | tf_op args[2]
  2.1 0.0 copy-start.6
  2.2 0.0 copy-done
  2.2 0.0 copy-done.1
  2.2 0.0 copy-done.2
  2.2 0.0 copy-done.3
  2.2 0.0 copy-done.4
  2.2 0.0 copy-done.5
  2.2 0.6 copy-done.6
  2.8 113.1 %shard_map.95 = (f32[160,256]{1,0:T(8,128)S(1)}, f32[64,256]{1,0:T(8,128)S(1)}) custom-call(s32[1,7]{1,0:T(1,128)S(1)} %copy-done.6, f32[160,256]{1,0:T(8,128)S(1)} %bitcast.12, f32[160,640]{1,0:T(8,128)S(1)} %bitcast.9, f32[896,160]{1,0:T(8,128)S(1)} %bitcast.8, s32[1,896]{1,0:T(1,128)S(1)} %copy-done.5, f32[64,256]{1,0:T(8,128)S(1)} %bitcast.14, ...), custom_call_target="tpu_custom_call" | custom-call | tf_op jit(solution)/shard_map/pallas_call | solution.py:436
  115.9 0.7 copy.13
  116.5 0.6 copy.14
Async XLA Ops:
  0.6 1.5 %copy-start = (f32[1,160,640]{2,1,0:T(8,128)S(1)}, f32[1,160,640]{2,1,0:T(8,128)}, u32[]{:S(2)}) copy-start(f32[1,160,640]{2,1,0:T(8,128)} %param.9) | copy-start | bytes 1228804
  0.6 1.5 %copy-start.1 = (f32[1,256,256]{2,1,0:T(8,128)S(1)}, f32[1,256,256]{2,1,0:T(8,128)}, u32[]{:S(2)}) copy-start(f32[1,256,256]{2,1,0:T(8,128)} %param.14) | copy-start | bytes 786436
  0.7 1.5 %copy-start.2 = (f32[1,256,256]{2,1,0:T(8,128)S(1)}, f32[1,256,256]{2,1,0:T(8,128)}, u32[]{:S(2)}) copy-start(f32[1,256,256]{2,1,0:T(8,128)} %param.15) | copy-start | bytes 786436
  0.7 1.5 %copy-start.3 = (f32[1,160,256]{2,1,0:T(8,128)S(1)}, f32[1,160,256]{2,1,0:T(8,128)}, u32[]{:S(2)}) copy-start(f32[1,160,256]{2,1,0:T(8,128)} %param.8) | copy-start | bytes 491524
  0.7 1.5 %copy-start.4 = (f32[1,64,256]{2,1,0:T(8,128)S(1)}, f32[1,64,256]{2,1,0:T(8,128)}, u32[]{:S(2)}) copy-start(f32[1,64,256]{2,1,0:T(8,128)} %param.13) | copy-start | bytes 196612
  0.7 1.5 %copy-start.5 = (s32[1,896]{1,0:T(1,128)S(1)}, s32[1,896]{1,0:T(1,128)}, u32[]{:S(2)}) copy-start(s32[1,896]{1,0:T(1,128)} %lists.1) | copy-start | bytes 10756
  2.1 0.7 copy-start.6

commit v2 on v0

v2 whole, which is shorter than its diff:
```python
import functools
import types

import jax
import jax.numpy as jnp
from jax import lax
from jax.experimental import pallas as pl
from jax.experimental.pallas import tpu as pltpu
from jax.sharding import PartitionSpec as P

MESH = pl.DeviceIdType.MESH
F32 = jnp.float32
BF16 = jnp.bfloat16
NSEP = 4


def split(x):
    high = x.astype(BF16)
    return high, (x - high.astype(F32)).astype(BF16)


def mm(a, b, ca=1, cb=0):
    return lax.dot_general(a, b, (((ca,), (cb,)), ((), ())), preferred_element_type=F32)


def mm3(a, b, ca=1, cb=0):
    ah, al = split(a)
    bh, bl = split(b)
    return mm(ah, bh, ca, cb) + (mm(al, bh, ca, cb) + mm(ah, bl, ca, cb))


def chain(rows, wh, wl):
    high, low = split(rows)
    m = rows.shape[0]
    both = mm(jnp.concatenate([high, low], axis=0), wh)
    return both[:m] + (both[m:] + mm(high, wl))


def picked_by(rows, picker, cb):
    high, low = split(rows)
    m = rows.shape[0]
    both = mm(jnp.concatenate([high, low], axis=0), picker, 1, cb)
    return both[:m] + both[m:]


def level_of(index, depth):
    level = jnp.int32(1)
    for k in range(1, depth + 1):
        level = level + (lax.rem(index, 2**k) == 0).astype(jnp.int32)
    return level


def kernel(dims, names, *refs):
    ny, nz, depth = dims
    b = types.SimpleNamespace(**dict(zip(names, refs)))
    kp = depth - nz.bit_length() + 1
    l = lax.axis_index("leaf")
    q = lax.axis_index("sep")
    c = lax.rem(l, 2)
    y = lax.rem(lax.div(l, 2), ny)
    z = lax.div(l, 2 * ny)
    pair = l + 1 - 2 * c
    rows = b.src.shape[0]
    cols = b.ssrc.shape[0]
    w = b.sinv.shape[0]
    cap = b.lists.shape[1] // depth
    rb = cols // ny
    mb = w // ny
    lam = level_of(l, depth)
    plane = level_of(z * 2 * ny, depth)
    core0 = c == 0
    core1 = c == 1
    owner = l > 0

    def when(*conditions):
        return pl.when(functools.reduce(jnp.logical_and, conditions))

    def at_sep(d):
        return (l, lax.rem(q + d, NSEP))

    def y_of(d):
        return lax.rem(y + d, ny)

    def z_of(d):
        return lax.rem(z + d, nz)

    def at_y(d):
        return (l - 2 * y + 2 * y_of(d), q)

    def at_z(d):
        return (l + 2 * ny * (z_of(d) - z), q)

    at_pair = (pair, q)

    def rcopy(a, dst, ss, rs, device):
        return pltpu.make_async_remote_copy(
            src_ref=a, dst_ref=dst, send_sem=ss, recv_sem=rs, device_id=device, device_id_type=MESH
        )

    drains = []

    def later(copy, *conditions):
        drains.append((copy, conditions))

    def ds(index, size):
        return pl.ds(pl.multiple_of(index * size, 8), size)

    barrier = pltpu.get_barrier_semaphore()
    greeted = [at_sep(d) for d in range(1, NSEP)] + [at_pair]
    greeted += [at_y(d) for d in range(1, ny)] + [at_z(d) for d in range(1, nz)]
    for device in greeted:
        pl.semaphore_signal(barrier, inc=1, device_id=device, device_id_type=MESH)

    own = ds(q, rows)
    mine = ds(q, cols)
    b.S[own, :] = b.src[...]
    for j in range(1, NSEP):

        @pl.when(j > q)
        def _():
            b.S[j * rows : (j + 1) * rows, :] = jnp.zeros((rows, b.S.shape[1]), F32)

    b.sp[...] = jnp.zeros_like(b.sp)
    b.sp[:, :cols] = b.ssrc[...].T
    b.ssb[q] = b.sp[mine, :]
    pl.semaphore_wait(barrier, len(greeted))

    def ag(d):
        return rcopy(b.S.at[own, :], b.S.at[own, :], b.agS.at[d], b.agR.at[d], at_sep(d))

    for d in (2, 1, 3):

        @pl.when(q + d < NSEP)
        def _():
            ag(d).start()

        later(functools.partial(ag, d), q + d < NSEP)

    def ssx(d):
        to = lax.rem(q + d, NSEP)
        return rcopy(b.sp.at[ds(to, cols), :], b.ssb.at[q], b.ssS.at[d], b.ssR.at[d], at_sep(d))

    for d in range(1, NSEP):
        ssx(d).start()
        later(functools.partial(ssx, d))

    sinv = b.sinv[...]
    b.Mo[...] = mm3(b.cpl[...], sinv)
    b.No[...] = mm3(sinv, sinv, 0, 0)

    def low_of(k, device, slot, m):
        src, dst = ((b.Mo, b.MB), (b.No, b.NB))[m]
        return rcopy(src, dst.at[k], b.moS.at[m, slot], b.mlR.at[m, k], device)

    def start_both(k, device, slot, *conditions):
        @when(*conditions)
        def _():
            for m in range(2):
                low_of(k, device, slot, m).start()

        for m in range(2):
            later(functools.partial(low_of, k, device, slot, m), *conditions)

    start_both(1, at_pair, 0, core1)
    for k in range(2, kp):
        reach = 2 ** (k - 2)
        slot = 0
        for o in range(-reach, reach):
            if o:
                start_both(k, (l + 2 * o, q), slot, core0, lam == k)
                slot += 1

    for k in range(1, kp):

        @when(lam == k)
        def _():
            b.MB[k] = b.Mo[...]
            b.NB[k] = b.No[...]

    def sc(m, d):
        src, dst = ((b.Mo, b.PM), (b.No, b.PN))[m]
        return rcopy(
            src.at[ds(y_of(d), mb), :], dst.at[lam], b.scS.at[m, d], b.scR.at[m, lam], at_y(d)
        )

    def wait_sc(m, k):
        dst = (b.PM, b.PN)[m]
        rcopy(dst.at[k], dst.at[k], b.scS.at[m, 0], b.scR.at[m, k], at_pair).wait_recv()

    high = jnp.logical_and(core0, jnp.logical_and(lam >= kp, owner))
    for m in range(2):
        has = (high, lam < depth) if m == 0 else (high,)

        @when(*has)
        def _():
            for d in range(1, ny):
                sc(m, d).start()
            dst, src = ((b.PM, b.Mo), (b.PN, b.No))[m]
            dst[lam] = src[ds(y, mb), :]

        for d in range(1, ny):
            later(functools.partial(sc, m, d), *has)

    wi = lax.broadcasted_iota(jnp.int32, (w, cap), 0)
    pi = lax.broadcasted_iota(jnp.int32, (w, cap), 1)
    for j in range(depth):
        hit = jnp.logical_and(wi == b.lists[0:1, j * cap : (j + 1) * cap], pi < b.counts[0, j])
        b.pick[j] = jnp.where(hit, 1.0, 0.0).astype(BF16)
    uh, ul = split(b.upd[...])
    b.updh[...] = uh
    b.updl[...] = ul

    def zm(m, d):
        dst = (b.PM, b.PN)[m]
        return rcopy(dst.at[plane], dst.at[plane], b.zmS.at[m, d], b.zmR.at[m, plane], at_z(d))

    def wait_zm(m, k):
        dst = (b.PM, b.PN)[m]
        rcopy(dst.at[k], dst.at[k], b.zmS.at[m, 0], b.zmR.at[m, k], at_pair).wait_recv()

    size = jnp.int32(1)
    for k in range(kp + 1, depth + 1):
        size = size + (plane >= k).astype(jnp.int32) * 2 ** (k - kp - 1)
    base = z - lax.div(size, 2)

    def in_node(d):
        zd = z_of(d)
        return jnp.logical_and(zd >= base, zd < base + size)

    for m in range(2):
        top = depth - 1 if m == 0 else depth

        @when(core0, y != ny // 2)
        def _():
            wait_sc(m, kp)

        @when(core0, y != 0, plane <= top)
        def _():
            wait_sc(m, plane)

        for d in range(1, nz):
            sends = (core0, plane <= top, in_node(d))

            @when(*sends)
            def _():
                zm(m, d).start()

            later(functools.partial(zm, m, d), *sends)

    def wait_low(k):
        for m, dst in enumerate((b.MB, b.NB)):
            rcopy(dst.at[k], dst.at[k], b.moS.at[m, 0], b.mlR.at[m, k], at_pair).wait_recv()

    def fw(m, lo, hi, i):
        dst = (b.MB, b.NB)[m]
        place = dst.at[lo:hi]
        return rcopy(place, place, b.fwS.at[m, i], b.fwR.at[m, i], at_pair)

    def forward(m, lo, hi, i):
        @when(core0)
        def _():
            fw(m, lo, hi, i).start()

        later(functools.partial(fw, m, lo, hi, i), core0)

    for k in range(2, kp):

        @when(core0, lam != k)
        def _():
            wait_low(k)

    if kp > 2:
        for m in range(2):
            forward(m, 2, kp, 0)

    for d in range(1, NSEP):

        @pl.when(q - d >= 0)
        def _():
            ag(d).wait_recv()

    b.yT[...] = mm3(b.inv[...], b.S[...]).T

    def rs(j, d):
        to = lax.rem(q + d, NSEP)
        return rcopy(
            b.TT.at[j, ds(to, cols), :], b.rsb.at[j, d], b.rsS.at[j, d], b.rsR.at[j, d], at_sep(d)
        )

    yh, yl = split(b.yT[...])
    for j in range(depth):
        bh = b.updh[:, j * cap : (j + 1) * cap]
        bl = b.updl[:, j * cap : (j + 1) * cap]
        b.TT[j] = mm(yh, bh) + (mm(yl, bh) + mm(yh, bl))
        for d in (2, 1, 3):
            rs(j, d).start()
            later(functools.partial(rs, j, d))

    def yg(m, d):
        dst, src = ((b.MB, b.PM), (b.NB, b.PN))[m]
        hi = depth if m == 0 else depth + 1
        return rcopy(
            src.at[kp:hi], dst.at[kp:hi, ds(y, mb), :], b.ygS.at[m, d], b.ygR.at[m, d], at_y(d)
        )

    for m in range(2):
        hi = depth if m == 0 else depth + 1

        @when(core0)
        def _():
            for k in range(kp + 1, hi):

                @pl.when(plane != k)
                def _():
                    wait_zm(m, k)

            for d in range(1, ny):
                yg(m, d).start()
            dst, src = ((b.MB, b.PM), (b.NB, b.PN))[m]
            dst[kp:hi, ds(y, mb), :] = src[kp:hi]

        for d in range(1, ny):
            later(functools.partial(yg, m, d), core0)

    for d in range(1, NSEP):
        ssx(d).wait_recv()
    sT = jnp.concatenate([b.ssb[i][:, :cols] for i in range(NSEP)], axis=1)
    b.sT[...] = sT

    def prepare(k):
        if k < depth:
            mh, ml = split(b.MB[k])
            b.Mh[k] = mh
            b.Ml[k] = ml
            th, tl = split(b.MB[k].T)
            b.Th[k] = th
            b.Tl[k] = tl

    def prepare_n(k):
        nh, nl = split(b.NB[k])
        b.Nh[k] = nh
        b.Nl[k] = nl

    @when(core0)
    def _():
        wait_low(1)

    if kp > 2:

        @when(core1)
        def _():
            for m in range(2):
                fw(m, 2, kp, 0).wait_recv()

    for k in range(1, kp):
        prepare(k)

    half = pl.ds(pl.multiple_of(c * 128, 128), 128)
    other = pl.ds(pl.multiple_of((1 - c) * 128, 128), 128)

    def own_part(k):
        for d in range(1, NSEP):
            rs(k - 1, d).wait_recv()
        t = (b.TT[k - 1, mine, :] + b.rsb[k - 1, 1]) + (b.rsb[k - 1, 2] + b.rsb[k - 1, 3])
        part = jnp.where(lam == k, b.sT[...], 0.0) - picked_by(t, b.pick[k - 1], 1)
        if k > 1:
            part = part - chain(b.RP[k - 1], b.Th[k - 1], b.Tl[k - 1])
        b.RP[k] = part

    def cx(i):
        if i == 0:
            return rcopy(b.RP.at[1], b.R1, b.cxS.at[0], b.cxR.at[0], at_pair)
        lo, hi = ((2, kp + 1), (kp + 1, depth + 1))[i - 1]
        return rcopy(
            b.RP.at[lo:hi, :, other], b.CX.at[lo:hi], b.cxS.at[i], b.cxR.at[i], at_pair
        )

    def hr(i, d):
        lo, hi = ((2, kp + 1), (kp + 1, depth + 1))[i]
        return rcopy(
            b.H.at[lo:hi, ds(y_of(d), rb), :],
            b.HR.at[y, lo:hi],
            b.hrS.at[i, d],
            b.hrR.at[i, d],
            at_y(d),
        )

    def plane_sums(i):
        lo, hi = ((2, kp + 1), (kp + 1, depth + 1))[i]
        cx(i + 1).wait_recv()
        b.H[lo:hi] = b.RP[lo:hi, :, half] + b.CX[lo:hi]
        for d in range(1, ny):
            hr(i, d).start()
            later(functools.partial(hr, i, d))
        b.HR[y, lo:hi] = b.H[lo:hi, ds(y, rb), :]

    own_part(1)
    cx(0).start()
    later(functools.partial(cx, 0))
    for k in range(2, kp + 1):
        own_part(k)
    cx(1).start()
    later(functools.partial(cx, 1))
    plane_sums(0)

    def high_matrices(m):
        hi = depth if m == 0 else depth + 1

        @when(core0)
        def _():
            for d in range(1, ny):
                yg(m, d).wait_recv()

        forward(m, kp, hi, 1)

        @when(core1)
        def _():
            fw(m, kp, hi, 1).wait_recv()

    high_matrices(0)
    for k in range(kp, depth):
        prepare(k)
    for k in range(kp + 1, depth + 1):
        own_part(k)
    cx(2).start()
    later(functools.partial(cx, 2))
    plane_sums(1)

    def br(d):
        return rcopy(
            b.B.at[y_of(d)],
            b.RF.at[2 : kp + 1, ds(y, rb), half],
            b.brS.at[0, d],
            b.brR.at[0, d],
            at_y(d),
        )

    def zr(d):
        return rcopy(b.ZT, b.ZR.at[z], b.zrS.at[d], b.zrR.at[d], at_z(d))

    def bz(d):
        return rcopy(
            b.BZ,
            b.RF.at[kp + 1 : depth + 1, ds(y, rb), half],
            b.brS.at[1, d],
            b.brR.at[1, d],
            at_y(d),
        )

    def back(i):
        lo, hi = ((2, kp + 1), (kp + 1, depth + 1))[i]
        place = b.RF.at[lo:hi, :, half]
        return rcopy(place, place, b.bkS.at[i], b.bkR.at[i], at_pair)

    for d in range(1, ny):
        hr(0, d).wait_recv()
    for k in range(2, kp + 1):
        step = 2 ** (k - 1)
        for g in range(0, ny, step):
            total = b.HR[g, k]
            for i in range(1, step):
                total = total + b.HR[g + i, k]
            for i in range(step):
                b.B[g + i, k - 2] = total
    for d in range(1, ny):
        br(d).start()
        later(functools.partial(br, d))
    b.RF[2 : kp + 1, ds(y, rb), half] = b.B[y]

    for d in range(1, ny):
        hr(1, d).wait_recv()
    total = b.HR[0, kp + 1 : depth + 1]
    for i in range(1, ny):
        total = total + b.HR[i, kp + 1 : depth + 1]
    b.ZT[...] = total
    for d in range(1, nz):
        zr(d).start()
        later(functools.partial(zr, d))
    b.ZR[z] = total

    cx(0).wait_recv()
    for d in range(1, ny):
        br(d).wait_recv()
    back(0).start()
    later(functools.partial(back, 0))
    for k in range(1, kp):
        prepare_n(k)
    high_matrices(1)
    for k in range(kp, depth + 1):
        prepare_n(k)
    back(0).wait_recv()
    b.RF[1] = b.RP[1] + b.R1[...]
    for k in range(1, kp + 1):
        b.V[k] = chain(b.RF[k], b.Nh[k], b.Nl[k])

    for d in range(1, nz):
        zr(d).wait_recv()
    for k in range(kp + 1, depth + 1):
        step = 2 ** (k - kp)
        first = z - lax.rem(z, step)
        total = b.ZR[first, k - kp - 1]
        for i in range(1, step):
            total = total + b.ZR[first + i, k - kp - 1]
        b.BZ[k - kp - 1] = total
    for d in range(1, ny):
        bz(d).start()
        later(functools.partial(bz, d))
    b.RF[kp + 1 : depth + 1, ds(y, rb), half] = b.BZ[...]
    for d in range(1, ny):
        bz(d).wait_recv()
    back(1).start()
    later(functools.partial(back, 1))
    back(1).wait_recv()

    def pk(j, d):
        place = b.pkb.at[mine, (j - 1) * cap : j * cap]
        return rcopy(place, place, b.pkS.at[j, d], b.pkR.at[j, d], at_sep(d))

    for k in range(kp + 1, depth + 1):
        b.V[k] = chain(b.RF[k], b.Nh[k], b.Nl[k])
    for j in range(depth, 0, -1):
        x = b.V[j]
        if j < depth:
            x = x - chain(b.X[j + 1], b.Mh[j], b.Ml[j])
        b.X[j] = x
        b.pkb[mine, (j - 1) * cap : j * cap] = picked_by(x, b.pick[j - 1], 0)
        for d in (2, 1, 3):
            pk(j, d).start()
            later(functools.partial(pk, j, d))

    def xo(d):
        to = lax.rem(q + d, NSEP)
        return rcopy(b.xp.at[ds(to, cols), :], b.xob.at[q], b.xS.at[d], b.xR.at[d], at_sep(d))

    b.xp[...] = jnp.zeros_like(b.xp)

    @when(owner)
    def _():
        b.xp[:, :cols] = b.X[lam].T

    b.xob[q] = b.xp[mine, :]
    for d in range(1, NSEP):
        xo(d).start()
        later(functools.partial(xo, d))

    for j in range(depth, 0, -1):
        for d in range(1, NSEP):
            pk(j, d).wait_recv()
    ph, pw = split(b.pkb[...])
    uh = b.updh[...]
    wT = b.yT[...] - (mm(ph, uh, 1, 1) + (mm(pw, uh, 1, 1) + mm(ph, b.updl[...], 1, 1)))
    b.XB[...] = mm3(b.inv[...], wT.T, 0, 0)

    def fin(d):
        to = q - d
        return rcopy(b.XB.at[ds(to, rows), :], b.fb.at[d], b.fS.at[d], b.fR.at[d], (l, to))

    for d in (2, 1, 3):

        @pl.when(q - d >= 0)
        def _():
            fin(d).start()

        later(functools.partial(fin, d), q - d >= 0)

    for d in range(1, NSEP):
        xo(d).wait_recv()
    b.sol[...] = jnp.concatenate([b.xob[i][:, :cols] for i in range(NSEP)], axis=1)
    b.out[...] = b.XB[own, :]
    for d in range(1, NSEP):

        @pl.when(q + d < NSEP)
        def _():
            rcopy(b.XB.at[own, :], b.fb.at[d], b.fS.at[d], b.fR.at[d], at_sep(d)).wait_recv()
            b.out[...] += b.fb[d]

    for copy, conditions in drains:
        if conditions:

            @when(*conditions)
            def _():
                copy().wait_send()

        else:
            copy().wait_send()


def per_device(ny, nz, src, inv, upd, lists, counts, ssrc, sinv, cpl):
    depth = counts.shape[1]
    rows, n = src.shape[1:]
    order = inv.shape[2]
    urows = upd.shape[1]
    cols = ssrc.shape[1]
    w = sinv.shape[1]
    cap = urows // depth
    s = depth + 1
    kp = depth - nz.bit_length() + 1
    rb = cols // ny
    mb = w // ny
    f = lambda *shape: pltpu.VMEM(shape, F32)
    h = lambda *shape: pltpu.VMEM(shape, BF16)
    dma = lambda *shape: pltpu.SemaphoreType.DMA(shape)
    vm = pl.BlockSpec(memory_space=pltpu.VMEM)
    scratch = dict(
        S=f(order, n),
        sp=f(n, 128),
        ssb=f(NSEP, cols, 128),
        sT=f(cols, w),
        Mo=f(w, w),
        No=f(w, w),
        MB=f(s, w, w),
        NB=f(s, w, w),
        PM=f(s, mb, w),
        PN=f(s, mb, w),
        Mh=h(s, w, w),
        Ml=h(s, w, w),
        Th=h(s, w, w),
        Tl=h(s, w, w),
        Nh=h(s, w, w),
        Nl=h(s, w, w),
        pick=h(depth, w, cap),
        yT=f(n, rows),
        updh=h(rows, urows),
        updl=h(rows, urows),
        TT=f(depth, n, cap),
        rsb=f(depth, NSEP, cols, cap),
        RP=f(s, cols, w),
        R1=f(cols, w),
        CX=f(s, cols, 128),
        H=f(s, cols, 128),
        HR=f(ny, s, rb, 128),
        B=f(ny, kp - 1, rb, 128),
        ZT=f(depth - kp, rb, 128),
        ZR=f(nz, depth - kp, rb, 128),
        BZ=f(depth - kp, rb, 128),
        RF=f(s, cols, w),
        V=f(s, cols, w),
        X=f(s, cols, w),
        pkb=f(n, urows),
        XB=f(order, n),
        fb=f(NSEP, rows, n),
        xp=f(n, 128),
        xob=f(NSEP, cols, 128),
        agS=dma(NSEP),
        agR=dma(NSEP),
        ssS=dma(NSEP),
        ssR=dma(NSEP),
        moS=dma(2, 8),
        mlR=dma(2, s),
        scS=dma(2, ny),
        scR=dma(2, s),
        zmS=dma(2, nz),
        zmR=dma(2, s),
        ygS=dma(2, ny),
        ygR=dma(2, ny),
        fwS=dma(2, 2),
        fwR=dma(2, 2),
        rsS=dma(depth, NSEP),
        rsR=dma(depth, NSEP),
        cxS=dma(3),
        cxR=dma(3),
        hrS=dma(2, ny),
        hrR=dma(2, ny),
        brS=dma(2, ny),
        brR=dma(2, ny),
        zrS=dma(nz),
        zrR=dma(nz),
        bkS=dma(2),
        bkR=dma(2),
        pkS=dma(s, NSEP),
        pkR=dma(s, NSEP),
        xS=dma(NSEP),
        xR=dma(NSEP),
        fS=dma(NSEP),
        fR=dma(NSEP),
    )
    operands = ["counts", "src", "inv", "upd", "lists", "ssrc", "sinv", "cpl", "out", "sol"]
    out, sol = pl.pallas_call(
        functools.partial(kernel, (ny, nz, depth), operands + list(scratch)),
        out_shape=(
            jax.ShapeDtypeStruct((rows, n), F32),
            jax.ShapeDtypeStruct((cols, n), F32),
        ),
        in_specs=[pl.BlockSpec(memory_space=pltpu.SMEM)] + [vm] * 7,
        out_specs=(vm, vm),
        scratch_shapes=list(scratch.values()),
        compiler_params=pltpu.CompilerParams(
            collective_id=0, has_side_effects=True, vmem_limit_bytes=48 * 2**20
        ),
    )(counts, src[0], inv[0], upd[0].T, lists, ssrc[0], sinv[0], cpl[0])
    return out[None], sol[None]


def solution(mesh):
    leaves = mesh.shape["leaf"]
    ny = nz = 8
    if leaves != 2 * ny * nz:
        ny, nz = (leaves // 4, 2)
    placed = (
        P("leaf", "sep", None),
        P("leaf", "sep", None),
        P("leaf", None, "sep"),
        P("leaf", None),
        P("leaf", None),
        P("leaf", "sep", None),
        P("leaf", None, None),
        P("leaf", None, None),
    )
    return jax.shard_map(
        functools.partial(per_device, ny, nz),
        mesh=mesh,
        in_specs=placed,
        out_specs=(P("leaf", "sep", None), P("leaf", "sep", None)),
        check_vma=False,
    )
```

time: 519 us -> 109 us (0.21)
  waiting for transfers between devices: 193 us -> 0 us
  blocking collectives: 140 us -> 0 us
  starting transfers between devices: 131 us -> 0 us
  Pallas kernels: 0 us -> 100 us
  matrix products: 21.9 us -> 0 us
  between operations: 15 us -> 0.66 us
  other arithmetic: 7.86 us -> 0 us
    all_gather x14 -> x0, blocking collectives: 140 us -> none  [the longest x13 129 us: sep_rows(): return lax.all_gather(payload, 'sep', axis=0, tiled=True)]
    ppermute x26 -> x0, starting transfers between devices: 131 us -> none  [passed_along(): return lax.ppermute(x, axis, pairs)]
    pallas_call x0 -> x1, Pallas kernels: none -> 100 us  [per_device(): pl.pallas_call(functools.partial(kernel, (ny, nz, depth), operands + list...]
    ppermute x26 -> x0, waiting for transfers between devices: 95.2 us -> none  [passed_along(): return lax.ppermute(x, axis, pairs)]
    reduce_scatter x1 -> x0, waiting for transfers between devices: 42.8 us -> none  [per_device(): lax.psum_scatter(densified, 'sep', scatter_dimension=0, tiled=True)]
    all_gather x1 -> x0, waiting for transfers between devices: 30.9 us -> none  [sep_rows(): return lax.all_gather(payload, 'sep', axis=0, tiled=True)]
    unnamed x4 -> x0, waiting for transfers between devices: 24.6 us -> none
    dot_general x32 -> x0, matrix products: 21.9 us -> none  [the longest x15 9.33 us: product_first(): lax.dot_general(matrix, operand, (((0,), (0,)), ((), ())), precision=high...]
  transfers between devices with their start and end apart: 29 -> 0, of which waited for: 27 -> 0; matrix products, arithmetic and copies ran while one was open for 0% -> 0% of each run, Pallas kernels for 0% -> 0%
where the time goes in v2:
time: 109 us; the launch traced here: 108 us
  Pallas kernels  100 us (92%)
  local copies, waits for them, and re-layouts  7.68 us (7%)
    pallas_call x1, Pallas kernels, per_device(): pl.pallas_call(functools.partial(kernel, (ny, nz, depth), operands + list...  100 us
    unnamed x18, local copies, waits for them, and re-layouts  7.68 us

profile of v2, /device:TPU:1, one launch (start us, length us, event | category | flops | bytes accessed | tf_op | source)
XLA Modules:
  0.0 108.4 jit_solution(6018679290319058126)
XLA Ops:
  0.6 0.0 copy-start.6
  0.6 0.0 copy-start.7
  0.7 0.7 copy-done.6
  1.3 0.0 copy-done.7
  1.3 0.0 copy-start
  1.3 1.1 copy-done
  2.4 0.0 copy-start.1
  2.4 1.0 copy-done.1
  3.4 0.0 copy-start.2
  3.4 0.9 copy-done.2
  4.3 0.0 copy-start.3
  4.3 0.9 copy-done.3
  5.3 0.0 copy-start.4
  5.3 0.9 copy-done.4
  6.2 0.0 copy-start.5
  6.2 0.8 copy-done.5
  7.0 100.0 %shard_map.95 = (f32[160,256]{1,0:T(8,128)S(1)}, f32[64,256]{1,0:T(8,128)S(1)}) custom-call(s32[1,7]{1,0:T(1,128)S(1)} %copy-done.7, f32[160,256]{1,0:T(8,128)S(1)} %bitcast.15, f32[160,640]{1,0:T(8,128)S(1)} %bitcast.11, f32[160,896]{1,0:T(8,128)S(1)} %bitcast.10, s32[1,896]{1,0:T(1,128)S(1)} %copy-done.6, f32[64,256]{1,0:T(8,128)S(1)} %bitcast.17, ...), custom_call_target="tpu_custom_call" | custom-call | tf_op jit(solution)/shard_map/pallas_call | solution.py:678
  107.1 0.7 copy.12
  107.7 0.6 copy.13
Async XLA Ops:
  0.6 0.7 copy-start.6
  0.6 0.7 copy-start.7
  1.3 1.1 copy-start
  2.4 1.0 copy-start.1
  3.4 0.9 copy-start.2
  4.3 0.9 copy-start.3
  5.3 0.9 copy-start.4
  6.2 0.8 copy-start.5

commit v3 on v2

--- a/solution.py
+++ b/solution.py
@@ -60,9 +60,9 @@
     y = lax.rem(lax.div(l, 2), ny)
     z = lax.div(l, 2 * ny)
     pair = l + 1 - 2 * c
-    rows = b.src.shape[0]
-    cols = b.ssrc.shape[0]
-    w = b.sinv.shape[0]
+    rows = b.xsrc.shape[0]
+    cols = b.xssrc.shape[0]
+    w = b.xsinv.shape[0]
     cap = b.lists.shape[1] // depth
     rb = cols // ny
     mb = w // ny
@@ -105,15 +105,28 @@
     def ds(index, size):
         return pl.ds(pl.multiple_of(index * size, 8), size)
 
+    own = ds(q, rows)
+    mine = ds(q, cols)
+    loads = {}
+    for i, (name, dst) in enumerate(
+        (
+            ("src", b.S.at[own, :]),
+            ("ssrc", b.ssrc),
+            ("sinv", b.sinv),
+            ("cpl", b.cpl),
+            ("inv", b.inv),
+            ("upd", b.upd),
+        )
+    ):
+        loads[name] = pltpu.make_async_copy(getattr(b, "x" + name), dst, b.ldS.at[i])
+        loads[name].start()
+
     barrier = pltpu.get_barrier_semaphore()
     greeted = [at_sep(d) for d in range(1, NSEP)] + [at_pair]
     greeted += [at_y(d) for d in range(1, ny)] + [at_z(d) for d in range(1, nz)]
     for device in greeted:
         pl.semaphore_signal(barrier, inc=1, device_id=device, device_id_type=MESH)
 
-    own = ds(q, rows)
-    mine = ds(q, cols)
-    b.S[own, :] = b.src[...]
     for j in range(1, NSEP):
 
         @pl.when(j > q)
@@ -121,8 +134,7 @@
             b.S[j * rows : (j + 1) * rows, :] = jnp.zeros((rows, b.S.shape[1]), F32)
 
     b.sp[...] = jnp.zeros_like(b.sp)
-    b.sp[:, :cols] = b.ssrc[...].T
-    b.ssb[q] = b.sp[mine, :]
+    loads["src"].wait()
     pl.semaphore_wait(barrier, len(greeted))
 
     def ag(d):
@@ -140,10 +152,15 @@
         to = lax.rem(q + d, NSEP)
         return rcopy(b.sp.at[ds(to, cols), :], b.ssb.at[q], b.ssS.at[d], b.ssR.at[d], at_sep(d))
 
+    loads["ssrc"].wait()
+    b.sp[:, :cols] = b.ssrc[...].T
+    b.ssb[q] = b.sp[mine, :]
     for d in range(1, NSEP):
         ssx(d).start()
         later(functools.partial(ssx, d))
 
+    loads["sinv"].wait()
+    loads["cpl"].wait()
     sinv = b.sinv[...]
     b.Mo[...] = mm3(b.cpl[...], sinv)
     b.No[...] = mm3(sinv, sinv, 0, 0)
@@ -206,6 +223,7 @@
     for j in range(depth):
         hit = jnp.logical_and(wi == b.lists[0:1, j * cap : (j + 1) * cap], pi < b.counts[0, j])
         b.pick[j] = jnp.where(hit, 1.0, 0.0).astype(BF16)
+    loads["upd"].wait()
     uh, ul = split(b.upd[...])
     b.updh[...] = uh
     b.updl[...] = ul
@@ -251,27 +269,25 @@
         for m, dst in enumerate((b.MB, b.NB)):
             rcopy(dst.at[k], dst.at[k], b.moS.at[m, 0], b.mlR.at[m, k], at_pair).wait_recv()
 
-    def fw(m, lo, hi, i):
-        dst = (b.MB, b.NB)[m]
-        place = dst.at[lo:hi]
-        return rcopy(place, place, b.fwS.at[m, i], b.fwR.at[m, i], at_pair)
-
-    def forward(m, lo, hi, i):
+    def fw(m):
+        place = (b.MB, b.NB)[m].at[2:kp]
+        return rcopy(place, place, b.fwS.at[m], b.fwR.at[m], at_pair)
+
+    for k in range(2, kp):
+
+        @when(core0, lam != k)
+        def _():
+            wait_low(k)
+
+    if kp > 2:
+
         @when(core0)
         def _():
-            fw(m, lo, hi, i).start()
-
-        later(functools.partial(fw, m, lo, hi, i), core0)
-
-    for k in range(2, kp):
-
-        @when(core0, lam != k)
-        def _():
-            wait_low(k)
-
-    if kp > 2:
+            for m in range(2):
+                fw(m).start()
+
         for m in range(2):
-            forward(m, 2, kp, 0)
+            later(functools.partial(fw, m), core0)
 
     for d in range(1, NSEP):
 
@@ -279,6 +295,7 @@
         def _():
             ag(d).wait_recv()
 
+    loads["inv"].wait()
     b.yT[...] = mm3(b.inv[...], b.S[...]).T
 
     def rs(j, d):
@@ -303,7 +320,7 @@
             src.at[kp:hi], dst.at[kp:hi, ds(y, mb), :], b.ygS.at[m, d], b.ygR.at[m, d], at_y(d)
         )
 
-    for m in range(2):
+    def gather_high(m):
         hi = depth if m == 0 else depth + 1
 
         @when(core0)
@@ -322,6 +339,7 @@
         for d in range(1, ny):
             later(functools.partial(yg, m, d), core0)
 
+    gather_high(0)
     for d in range(1, NSEP):
         ssx(d).wait_recv()
     sT = jnp.concatenate([b.ssb[i][:, :cols] for i in range(NSEP)], axis=1)
@@ -350,33 +368,34 @@
         @when(core1)
         def _():
             for m in range(2):
-                fw(m, 2, kp, 0).wait_recv()
+                fw(m).wait_recv()
 
     for k in range(1, kp):
         prepare(k)
 
-    half = pl.ds(pl.multiple_of(c * 128, 128), 128)
-    other = pl.ds(pl.multiple_of((1 - c) * 128, 128), 128)
 
     def own_part(k):
         for d in range(1, NSEP):
             rs(k - 1, d).wait_recv()
         t = (b.TT[k - 1, mine, :] + b.rsb[k - 1, 1]) + (b.rsb[k - 1, 2] + b.rsb[k - 1, 3])
         part = jnp.where(lam == k, b.sT[...], 0.0) - picked_by(t, b.pick[k - 1], 1)
-        if k > 1:
+        if 1 < k <= kp:
             part = part - chain(b.RP[k - 1], b.Th[k - 1], b.Tl[k - 1])
         b.RP[k] = part
 
+    groups = ((2, kp), (kp, depth), (depth, depth + 1))
+    sums_on = (core1, core0, core0)
+    sends_to_pair = (core0, core1, core1)
+
+    def r1():
+        return rcopy(b.RP.at[1], b.R1, b.cxS.at[3], b.cxR.at[3], at_pair)
+
     def cx(i):
-        if i == 0:
-            return rcopy(b.RP.at[1], b.R1, b.cxS.at[0], b.cxR.at[0], at_pair)
-        lo, hi = ((2, kp + 1), (kp + 1, depth + 1))[i - 1]
-        return rcopy(
-            b.RP.at[lo:hi, :, other], b.CX.at[lo:hi], b.cxS.at[i], b.cxR.at[i], at_pair
-        )
+        lo, hi = groups[i]
+        return rcopy(b.RP.at[lo:hi], b.CX.at[lo:hi], b.cxS.at[i], b.cxR.at[i], at_pair)
 
     def hr(i, d):
-        lo, hi = ((2, kp + 1), (kp + 1, depth + 1))[i]
+        lo, hi = groups[i]
         return rcopy(
             b.H.at[lo:hi, ds(y_of(d), rb), :],
             b.HR.at[y, lo:hi],
@@ -385,144 +404,158 @@
             at_y(d),
         )
 
-    def plane_sums(i):
-        lo, hi = ((2, kp + 1), (kp + 1, depth + 1))[i]
-        cx(i + 1).wait_recv()
-        b.H[lo:hi] = b.RP[lo:hi, :, half] + b.CX[lo:hi]
-        for d in range(1, ny):
-            hr(i, d).start()
-            later(functools.partial(hr, i, d))
-        b.HR[y, lo:hi] = b.H[lo:hi, ds(y, rb), :]
+    def share(i):
+        @when(sends_to_pair[i])
+        def _():
+            cx(i).start()
+
+        later(functools.partial(cx, i), sends_to_pair[i])
+
+        @when(sums_on[i])
+        def _():
+            lo, hi = groups[i]
+            cx(i).wait_recv()
+            b.H[lo:hi] = b.RP[lo:hi] + b.CX[lo:hi]
+            for d in range(1, ny):
+                hr(i, d).start()
+            b.HR[y, lo:hi] = b.H[lo:hi, ds(y, rb), :]
+
+        for d in range(1, ny):
+            later(functools.partial(hr, i, d), sums_on[i])
 
     own_part(1)
-    cx(0).start()
-    later(functools.partial(cx, 0))
-    for k in range(2, kp + 1):
+    r1().start()
+    later(r1)
+    for k in range(2, kp):
         own_part(k)
-    cx(1).start()
-    later(functools.partial(cx, 1))
-    plane_sums(0)
-
-    def high_matrices(m):
-        hi = depth if m == 0 else depth + 1
-
-        @when(core0)
-        def _():
-            for d in range(1, ny):
-                yg(m, d).wait_recv()
-
-        forward(m, kp, hi, 1)
-
-        @when(core1)
-        def _():
-            fw(m, kp, hi, 1).wait_recv()
-
-    high_matrices(0)
+    share(0)
     for k in range(kp, depth):
-        prepare(k)
-    for k in range(kp + 1, depth + 1):
         own_part(k)
-    cx(2).start()
-    later(functools.partial(cx, 2))
-    plane_sums(1)
+    share(1)
+    own_part(depth)
+    share(2)
+    gather_high(1)
 
     def br(d):
-        return rcopy(
-            b.B.at[y_of(d)],
-            b.RF.at[2 : kp + 1, ds(y, rb), half],
-            b.brS.at[0, d],
-            b.brR.at[0, d],
-            at_y(d),
-        )
+        place = b.RF.at[2:kp, ds(y, rb), :]
+        return rcopy(b.B.at[y_of(d)], place, b.brS.at[d], b.brR.at[d], at_y(d))
 
     def zr(d):
         return rcopy(b.ZT, b.ZR.at[z], b.zrS.at[d], b.zrR.at[d], at_z(d))
 
     def bz(d):
-        return rcopy(
-            b.BZ,
-            b.RF.at[kp + 1 : depth + 1, ds(y, rb), half],
-            b.brS.at[1, d],
-            b.brR.at[1, d],
-            at_y(d),
-        )
-
-    def back(i):
-        lo, hi = ((2, kp + 1), (kp + 1, depth + 1))[i]
-        place = b.RF.at[lo:hi, :, half]
-        return rcopy(place, place, b.bkS.at[i], b.bkR.at[i], at_pair)
+        place = b.X.at[kp : depth + 1, ds(y, rb), :]
+        return rcopy(b.BZ, place, b.bzS.at[d], b.bzR.at[d], at_y(d))
+
+    def back_low():
+        place = b.RF.at[2:kp]
+        return rcopy(place, place, b.bkS.at[0], b.bkR.at[0], at_pair)
+
+    def back_high():
+        place = b.X.at[kp : depth + 1]
+        return rcopy(place, place, b.bkS.at[1], b.bkR.at[1], at_pair)
+
+    @when(core1)
+    def _():
+        for d in range(1, ny):
+            hr(0, d).wait_recv()
+        for k in range(2, kp):
+            step = 2 ** (k - 1)
+            for g in range(0, ny, step):
+                total = b.HR[g, k]
+                for i in range(1, step):
+                    total = total + b.HR[g + i, k]
+                for i in range(step):
+                    b.B[g + i, k - 2] = total
+        for d in range(1, ny):
+            br(d).start()
+        b.RF[2:kp, ds(y, rb), :] = b.B[y]
+        for d in range(1, ny):
+            br(d).wait_recv()
+        back_low().start()
 
     for d in range(1, ny):
-        hr(0, d).wait_recv()
-    for k in range(2, kp + 1):
-        step = 2 ** (k - 1)
-        for g in range(0, ny, step):
-            total = b.HR[g, k]
-            for i in range(1, step):
-                total = total + b.HR[g + i, k]
-            for i in range(step):
-                b.B[g + i, k - 2] = total
-    for d in range(1, ny):
-        br(d).start()
-        later(functools.partial(br, d))
-    b.RF[2 : kp + 1, ds(y, rb), half] = b.B[y]
-
-    for d in range(1, ny):
-        hr(1, d).wait_recv()
-    total = b.HR[0, kp + 1 : depth + 1]
-    for i in range(1, ny):
-        total = total + b.HR[i, kp + 1 : depth + 1]
-    b.ZT[...] = total
+        later(functools.partial(br, d), core1)
+    later(back_low, core1)
+
+    @when(core0)
+    def _():
+        for d in range(1, ny):
+            yg(0, d).wait_recv()
+        for k in range(kp, depth):
+            prepare(k)
+        for i in (1, 2):
+            for d in range(1, ny):
+                hr(i, d).wait_recv()
+        for k in range(kp, depth + 1):
+            total = b.HR[0, k]
+            for i in range(1, ny):
+                total = total + b.HR[i, k]
+            if k > kp:
+                total = total - chain(b.RZ[k - 1], b.Th[k - 1], b.Tl[k - 1])
+                b.ZT[k - kp - 1] = total
+            b.RZ[k] = total
+        for d in range(1, nz):
+            zr(d).start()
+        b.ZR[z] = b.ZT[...]
+
     for d in range(1, nz):
-        zr(d).start()
-        later(functools.partial(zr, d))
-    b.ZR[z] = total
-
-    cx(0).wait_recv()
-    for d in range(1, ny):
-        br(d).wait_recv()
-    back(0).start()
-    later(functools.partial(back, 0))
+        later(functools.partial(zr, d), core0)
+
     for k in range(1, kp):
         prepare_n(k)
-    high_matrices(1)
-    for k in range(kp, depth + 1):
-        prepare_n(k)
-    back(0).wait_recv()
+    r1().wait_recv()
     b.RF[1] = b.RP[1] + b.R1[...]
-    for k in range(1, kp + 1):
+
+    @when(core0)
+    def _():
+        back_low().wait_recv()
+
+    for k in range(1, kp):
         b.V[k] = chain(b.RF[k], b.Nh[k], b.Nl[k])
 
-    for d in range(1, nz):
-        zr(d).wait_recv()
-    for k in range(kp + 1, depth + 1):
-        step = 2 ** (k - kp)
-        first = z - lax.rem(z, step)
-        total = b.ZR[first, k - kp - 1]
-        for i in range(1, step):
-            total = total + b.ZR[first + i, k - kp - 1]
-        b.BZ[k - kp - 1] = total
+    @when(core0)
+    def _():
+        for d in range(1, ny):
+            yg(1, d).wait_recv()
+        for k in range(kp, depth + 1):
+            prepare_n(k)
+        for d in range(1, nz):
+            zr(d).wait_recv()
+        for k in range(kp + 1, depth + 1):
+            step = 2 ** (k - kp)
+            first = z - lax.rem(z, step)
+            total = b.ZR[first, k - kp - 1]
+            for i in range(1, step):
+                total = total + b.ZR[first + i, k - kp - 1]
+            b.RZ[k] = total
+        for k in range(kp, depth + 1):
+            b.BZ[k - kp] = chain(b.RZ[k], b.Nh[k], b.Nl[k])
+        for k in range(depth - 1, kp - 1, -1):
+            b.BZ[k - kp] = b.BZ[k - kp] - chain(b.BZ[k + 1 - kp], b.Mh[k], b.Ml[k])
+        for d in range(1, ny):
+            bz(d).start()
+        b.X[kp : depth + 1, ds(y, rb), :] = b.BZ[...]
+        for d in range(1, ny):
+            bz(d).wait_recv()
+        back_high().start()
+
     for d in range(1, ny):
-        bz(d).start()
-        later(functools.partial(bz, d))
-    b.RF[kp + 1 : depth + 1, ds(y, rb), half] = b.BZ[...]
-    for d in range(1, ny):
-        bz(d).wait_recv()
-    back(1).start()
-    later(functools.partial(back, 1))
-    back(1).wait_recv()
+        later(functools.partial(bz, d), core0)
+    later(back_high, core0)
+
+    @when(core1)
+    def _():
+        back_high().wait_recv()
 
     def pk(j, d):
         place = b.pkb.at[mine, (j - 1) * cap : j * cap]
         return rcopy(place, place, b.pkS.at[j, d], b.pkR.at[j, d], at_sep(d))
 
-    for k in range(kp + 1, depth + 1):
-        b.V[k] = chain(b.RF[k], b.Nh[k], b.Nl[k])
-    for j in range(depth, 0, -1):
-        x = b.V[j]
-        if j < depth:
-            x = x - chain(b.X[j + 1], b.Mh[j], b.Ml[j])
-        b.X[j] = x
+    for j in list(range(kp - 1, 0, -1)) + list(range(depth, kp - 1, -1)):
+        if j < kp:
+            b.X[j] = b.V[j] - chain(b.X[j + 1], b.Mh[j], b.Ml[j])
+        x = b.X[j]
         b.pkb[mine, (j - 1) * cap : j * cap] = picked_by(x, b.pick[j - 1], 0)
         for d in (2, 1, 3):
             pk(j, d).start()
@@ -601,7 +634,14 @@
     h = lambda *shape: pltpu.VMEM(shape, BF16)
     dma = lambda *shape: pltpu.SemaphoreType.DMA(shape)
     vm = pl.BlockSpec(memory_space=pltpu.VMEM)
+    hbm = pl.BlockSpec(memory_space=pl.ANY)
     scratch = dict(
+        ssrc=f(cols, n),
+        sinv=f(w, w),
+        cpl=f(w, w),
+        inv=f(rows, order),
+        upd=f(rows, urows),
+        ldS=dma(6),
         S=f(order, n),
         sp=f(n, 128),
         ssb=f(NSEP, cols, 128),
@@ -626,15 +666,16 @@
         rsb=f(depth, NSEP, cols, cap),
         RP=f(s, cols, w),
         R1=f(cols, w),
-        CX=f(s, cols, 128),
-        H=f(s, cols, 128),
-        HR=f(ny, s, rb, 128),
-        B=f(ny, kp - 1, rb, 128),
-        ZT=f(depth - kp, rb, 128),
-        ZR=f(nz, depth - kp, rb, 128),
-        BZ=f(depth - kp, rb, 128),
-        RF=f(s, cols, w),
-        V=f(s, cols, w),
+        CX=f(s, cols, w),
+        H=f(s, cols, w),
+        HR=f(ny, s, rb, w),
+        B=f(ny, kp - 2, rb, w),
+        RZ=f(s, rb, w),
+        ZT=f(depth - kp, rb, w),
+        ZR=f(nz, depth - kp, rb, w),
+        BZ=f(depth - kp + 1, rb, w),
+        RF=f(kp, cols, w),
+        V=f(kp, cols, w),
         X=f(s, cols, w),
         pkb=f(n, urows),
         XB=f(order, n),
@@ -653,16 +694,18 @@
         zmR=dma(2, s),
         ygS=dma(2, ny),
         ygR=dma(2, ny),
-        fwS=dma(2, 2),
-        fwR=dma(2, 2),
+        fwS=dma(2),
+        fwR=dma(2),
         rsS=dma(depth, NSEP),
         rsR=dma(depth, NSEP),
-        cxS=dma(3),
-        cxR=dma(3),
-        hrS=dma(2, ny),
-        hrR=dma(2, ny),
-        brS=dma(2, ny),
-        brR=dma(2, ny),
+        cxS=dma(4),
+        cxR=dma(4),
+        hrS=dma(3, ny),
+        hrR=dma(3, ny),
+        brS=dma(ny),
+        brR=dma(ny),
+        bzS=dma(ny),
+        bzR=dma(ny),
         zrS=dma(nz),
         zrR=dma(nz),
         bkS=dma(2),
@@ -674,18 +717,18 @@
         fS=dma(NSEP),
         fR=dma(NSEP),
     )
-    operands = ["counts", "src", "inv", "upd", "lists", "ssrc", "sinv", "cpl", "out", "sol"]
+    operands = ["counts", "xsrc", "xinv", "xupd", "lists", "xssrc", "xsinv", "xcpl", "out", "sol"]
     out, sol = pl.pallas_call(
         functools.partial(kernel, (ny, nz, depth), operands + list(scratch)),
         out_shape=(
             jax.ShapeDtypeStruct((rows, n), F32),
             jax.ShapeDtypeStruct((cols, n), F32),
         ),
-        in_specs=[pl.BlockSpec(memory_space=pltpu.SMEM)] + [vm] * 7,
+        in_specs=[pl.BlockSpec(memory_space=pltpu.SMEM)] + [hbm] * 3 + [vm] + [hbm] * 3,
         out_specs=(vm, vm),
         scratch_shapes=list(scratch.values()),
         compiler_params=pltpu.CompilerParams(
-            collective_id=0, has_side_effects=True, vmem_limit_bytes=48 * 2**20
+            collective_id=0, has_side_effects=True, vmem_limit_bytes=62 * 2**20
         ),
     )(counts, src[0], inv[0], upd[0].T, lists, ssrc[0], sinv[0], cpl[0])
     return out[None], sol[None]

time: 109 us -> 101 us (0.927)
  local copies, waits for them, and re-layouts: 7.68 us -> 2.26 us
  Pallas kernels: 100 us -> 97.7 us
    unnamed x18 -> x4, local copies, waits for them, and re-layouts: 7.68 us -> 2.26 us
    pallas_call x1, Pallas kernels: 100 us -> 97.7 us  [per_device(): pl.pallas_call(functools.partial(kernel, (ny, nz, depth), operands + list...]
where the time goes in v3:
time: 101 us
  Pallas kernels  97.7 us (97%)
  local copies, waits for them, and re-layouts  2.26 us (2%)
    pallas_call x1, Pallas kernels, per_device(): pl.pallas_call(functools.partial(kernel, (ny, nz, depth), operands + list...  97.7 us
    unnamed x4, local copies, waits for them, and re-layouts  2.26 us

profile of v3, /device:TPU:1, one launch (start us, length us, event | category | flops | bytes accessed | tf_op | source)
XLA Modules:
  0.0 100.6 jit_solution(6575662741047719610)
XLA Ops:
  0.6 97.7 %shard_map.95 = (f32[160,256]{1,0:T(8,128)}, f32[64,256]{1,0:T(8,128)}) custom-call(s32[1,7]{1,0:T(1,128)} %refs_0_.1, f32[160,256]{1,0:T(8,128)} %bitcast.15, f32[160,640]{1,0:T(8,128)} %bitcast.11, f32[160,896]{1,0:T(8,128)} %bitcast.10, s32[1,896]{1,0:T(1,128)} %refs_4_.1, f32[64,256]{1,0:T(8,128)} %bitcast.17, f32[256,256]{1,0:T(8,128)} %bitcast.12, ...), custom_call_target="tpu_custom_call" | custom-call | tf_op jit(solution)/shard_map/pallas_call | solution.py:721
  98.4 0.0 copy-start
  98.4 1.6 %copy.12 = f32[1,160,256]{2,1,0:T(8,128)} copy(f32[1,160,256]{2,1,0:T(8,128)} %bitcast.14) | data formatting | bytes 327680
  100.0 0.0 copy-done
  100.0 0.6 copy.13
Async XLA Ops:
  98.4 1.6 %copy-start = (f32[64,256]{1,0:T(8,128)S(1)}, f32[64,256]{1,0:T(8,128)}, u32[]{:S(2)}) copy-start(f32[64,256]{1,0:T(8,128)} %get-tuple-element.5) | copy-start | bytes 196612

commit v4 on v3

--- a/solution.py
+++ b/solution.py
@@ -65,12 +65,15 @@
     w = b.xsinv.shape[0]
     cap = b.lists.shape[1] // depth
     rb = cols // ny
+    rh = 2 * rb
     mb = w // ny
     lam = level_of(l, depth)
     plane = level_of(z * 2 * ny, depth)
     core0 = c == 0
     core1 = c == 1
     owner = l > 0
+    even_y = lax.rem(y, 2) == 0
+    solver = jnp.logical_and(core0, even_y)
 
     def when(*conditions):
         return pl.when(functools.reduce(jnp.logical_and, conditions))
@@ -83,6 +86,9 @@
 
     def z_of(d):
         return lax.rem(z + d, nz)
+
+    def even_at(d):
+        return lax.rem(y + d, 2) == 0
 
     def at_y(d):
         return (l - 2 * y + 2 * y_of(d), q)
@@ -332,12 +338,18 @@
                     wait_zm(m, k)
 
             for d in range(1, ny):
-                yg(m, d).start()
+
+                @pl.when(even_at(d))
+                def _():
+                    yg(m, d).start()
+
+        for d in range(1, ny):
+            later(functools.partial(yg, m, d), core0, even_at(d))
+
+        @when(solver)
+        def _():
             dst, src = ((b.MB, b.PM), (b.NB, b.PN))[m]
             dst[kp:hi, ds(y, mb), :] = src[kp:hi]
-
-        for d in range(1, ny):
-            later(functools.partial(yg, m, d), core0)
 
     gather_high(0)
     for d in range(1, NSEP):
@@ -396,15 +408,16 @@
 
     def hr(i, d):
         lo, hi = groups[i]
-        return rcopy(
-            b.H.at[lo:hi, ds(y_of(d), rb), :],
-            b.HR.at[y, lo:hi],
-            b.hrS.at[i, d],
-            b.hrR.at[i, d],
-            at_y(d),
-        )
+        if i == 0:
+            src, dst = b.H.at[lo:hi, ds(y_of(d), rb), :], b.HR.at[y]
+        else:
+            src = b.H.at[lo:hi, ds(lax.div(y_of(d), 2), rh), :]
+            dst = b.HH.at[y, lo - kp : hi - kp]
+        return rcopy(src, dst, b.hrS.at[i, d], b.hrR.at[i, d], at_y(d))
 
     def share(i):
+        lo, hi = groups[i]
+
         @when(sends_to_pair[i])
         def _():
             cx(i).start()
@@ -413,15 +426,28 @@
 
         @when(sums_on[i])
         def _():
-            lo, hi = groups[i]
             cx(i).wait_recv()
             b.H[lo:hi] = b.RP[lo:hi] + b.CX[lo:hi]
             for d in range(1, ny):
-                hr(i, d).start()
-            b.HR[y, lo:hi] = b.H[lo:hi, ds(y, rb), :]
+                if i == 0:
+                    hr(i, d).start()
+                else:
+
+                    @pl.when(even_at(d))
+                    def _():
+                        hr(i, d).start()
+
+            if i == 0:
+                b.HR[y] = b.H[lo:hi, ds(y, rb), :]
+
+        if i:
+
+            @when(solver)
+            def _():
+                b.HH[y, lo - kp : hi - kp] = b.H[lo:hi, ds(lax.div(y, 2), rh), :]
 
         for d in range(1, ny):
-            later(functools.partial(hr, i, d), sums_on[i])
+            later(functools.partial(hr, i, d), sums_on[i], *((even_at(d),) if i else ()))
 
     own_part(1)
     r1().start()
@@ -440,20 +466,29 @@
         place = b.RF.at[2:kp, ds(y, rb), :]
         return rcopy(b.B.at[y_of(d)], place, b.brS.at[d], b.brR.at[d], at_y(d))
 
-    def zr(d):
-        return rcopy(b.ZT, b.ZR.at[z], b.zrS.at[d], b.zrR.at[d], at_z(d))
-
-    def bz(d):
-        place = b.X.at[kp : depth + 1, ds(y, rb), :]
-        return rcopy(b.BZ, place, b.bzS.at[d], b.bzR.at[d], at_y(d))
+    def z_xor(i):
+        other = z
+        for bit in range(nz.bit_length() - 1):
+            if i >> bit & 1:
+                other = other + 2**bit - 2 ** (bit + 1) * lax.rem(lax.div(z, 2**bit), 2)
+        return other
+
+    def zr(k, i):
+        device = (l + 2 * ny * (z_xor(i) - z), q)
+        at = k - kp - 1
+        return rcopy(b.ZT.at[at], b.ZR.at[at, z], b.zrS.at[at, i], b.zrR.at[at, i], device)
+
+    def bz(k, d):
+        place = b.X.at[k, ds(lax.div(y, 2), rh), :]
+        return rcopy(b.BZ.at[k - kp], place, b.bzS.at[k - kp, d], b.bzR.at[k - kp, d], at_y(d))
 
     def back_low():
         place = b.RF.at[2:kp]
         return rcopy(place, place, b.bkS.at[0], b.bkR.at[0], at_pair)
 
-    def back_high():
-        place = b.X.at[kp : depth + 1]
-        return rcopy(place, place, b.bkS.at[1], b.bkR.at[1], at_pair)
+    def back_high(k):
+        place = b.X.at[k]
+        return rcopy(place, place, b.bkS.at[k], b.bkR.at[k], at_pair)
 
     @when(core1)
     def _():
@@ -462,9 +497,9 @@
         for k in range(2, kp):
             step = 2 ** (k - 1)
             for g in range(0, ny, step):
-                total = b.HR[g, k]
+                total = b.HR[g, k - 2]
                 for i in range(1, step):
-                    total = total + b.HR[g + i, k]
+                    total = total + b.HR[g + i, k - 2]
                 for i in range(step):
                     b.B[g + i, k - 2] = total
         for d in range(1, ny):
@@ -478,29 +513,30 @@
         later(functools.partial(br, d), core1)
     later(back_low, core1)
 
-    @when(core0)
+    @when(solver)
     def _():
         for d in range(1, ny):
             yg(0, d).wait_recv()
         for k in range(kp, depth):
             prepare(k)
-        for i in (1, 2):
-            for d in range(1, ny):
-                hr(i, d).wait_recv()
         for k in range(kp, depth + 1):
-            total = b.HR[0, k]
+            if k == kp or k == depth:
+                for d in range(1, ny):
+                    hr(1 if k == kp else 2, d).wait_recv()
+            total = b.HH[0, k - kp]
             for i in range(1, ny):
-                total = total + b.HR[i, k]
+                total = total + b.HH[i, k - kp]
             if k > kp:
                 total = total - chain(b.RZ[k - 1], b.Th[k - 1], b.Tl[k - 1])
                 b.ZT[k - kp - 1] = total
+                for i in range(1, 2 ** (k - kp)):
+                    zr(k, i).start()
+                b.ZR[k - kp - 1, z] = total
             b.RZ[k] = total
-        for d in range(1, nz):
-            zr(d).start()
-        b.ZR[z] = b.ZT[...]
-
-    for d in range(1, nz):
-        later(functools.partial(zr, d), core0)
+
+    for k in range(kp + 1, depth + 1):
+        for i in range(1, 2 ** (k - kp)):
+            later(functools.partial(zr, k, i), solver)
 
     for k in range(1, kp):
         prepare_n(k)
@@ -514,52 +550,66 @@
     for k in range(1, kp):
         b.V[k] = chain(b.RF[k], b.Nh[k], b.Nl[k])
 
-    @when(core0)
+    @when(solver)
     def _():
         for d in range(1, ny):
             yg(1, d).wait_recv()
         for k in range(kp, depth + 1):
             prepare_n(k)
-        for d in range(1, nz):
-            zr(d).wait_recv()
-        for k in range(kp + 1, depth + 1):
-            step = 2 ** (k - kp)
-            first = z - lax.rem(z, step)
-            total = b.ZR[first, k - kp - 1]
-            for i in range(1, step):
-                total = total + b.ZR[first + i, k - kp - 1]
-            b.RZ[k] = total
         for k in range(kp, depth + 1):
-            b.BZ[k - kp] = chain(b.RZ[k], b.Nh[k], b.Nl[k])
-        for k in range(depth - 1, kp - 1, -1):
-            b.BZ[k - kp] = b.BZ[k - kp] - chain(b.BZ[k + 1 - kp], b.Mh[k], b.Ml[k])
+            total = b.RZ[k]
+            if k > kp:
+                step = 2 ** (k - kp)
+                for i in range(1, step):
+                    zr(k, i).wait_recv()
+                first = z - lax.rem(z, step)
+                total = b.ZR[k - kp - 1, first]
+                for i in range(1, step):
+                    total = total + b.ZR[k - kp - 1, first + i]
+            b.BZ[k - kp] = chain(total, b.Nh[k], b.Nl[k])
+        for k in range(depth, kp - 1, -1):
+            if k < depth:
+                b.BZ[k - kp] = b.BZ[k - kp] - chain(b.BZ[k + 1 - kp], b.Mh[k], b.Ml[k])
+            for d in range(1, ny):
+                bz(k, d).start()
+            b.X[k, ds(lax.div(y, 2), rh), :] = b.BZ[k - kp]
+
+    def arrive(k):
+        @when(core0)
+        def _():
+            for d in range(1, ny):
+
+                @pl.when(even_at(d))
+                def _():
+                    bz(k, d).wait_recv()
+
+            back_high(k).start()
+
+        @when(core1)
+        def _():
+            back_high(k).wait_recv()
+
+    for k in range(kp, depth + 1):
         for d in range(1, ny):
-            bz(d).start()
-        b.X[kp : depth + 1, ds(y, rb), :] = b.BZ[...]
-        for d in range(1, ny):
-            bz(d).wait_recv()
-        back_high().start()
-
-    for d in range(1, ny):
-        later(functools.partial(bz, d), core0)
-    later(back_high, core0)
-
-    @when(core1)
-    def _():
-        back_high().wait_recv()
+            later(functools.partial(bz, k, d), solver)
+        later(functools.partial(back_high, k), core0)
 
     def pk(j, d):
         place = b.pkb.at[mine, (j - 1) * cap : j * cap]
         return rcopy(place, place, b.pkS.at[j, d], b.pkR.at[j, d], at_sep(d))
 
-    for j in list(range(kp - 1, 0, -1)) + list(range(depth, kp - 1, -1)):
-        if j < kp:
-            b.X[j] = b.V[j] - chain(b.X[j + 1], b.Mh[j], b.Ml[j])
-        x = b.X[j]
-        b.pkb[mine, (j - 1) * cap : j * cap] = picked_by(x, b.pick[j - 1], 0)
+    def send_picked(j):
+        b.pkb[mine, (j - 1) * cap : j * cap] = picked_by(b.X[j], b.pick[j - 1], 0)
         for d in (2, 1, 3):
             pk(j, d).start()
             later(functools.partial(pk, j, d))
+
+    for j in range(depth, 0, -1):
+        if j >= kp:
+            arrive(j)
+        if j <= kp and j > 1:
+            b.X[j - 1] = b.V[j - 1] - chain(b.X[j], b.Mh[j - 1], b.Ml[j - 1])
+        send_picked(j)
 
     def xo(d):
         to = lax.rem(q + d, NSEP)
@@ -668,12 +718,13 @@
         R1=f(cols, w),
         CX=f(s, cols, w),
         H=f(s, cols, w),
-        HR=f(ny, s, rb, w),
+        HR=f(ny, kp - 2, rb, w),
+        HH=f(ny, depth - kp + 1, 2 * rb, w),
         B=f(ny, kp - 2, rb, w),
-        RZ=f(s, rb, w),
-        ZT=f(depth - kp, rb, w),
-        ZR=f(nz, depth - kp, rb, w),
-        BZ=f(depth - kp + 1, rb, w),
+        RZ=f(s, 2 * rb, w),
+        ZT=f(depth - kp, 2 * rb, w),
+        ZR=f(depth - kp, nz, 2 * rb, w),
+        BZ=f(depth - kp + 1, 2 * rb, w),
         RF=f(kp, cols, w),
         V=f(kp, cols, w),
         X=f(s, cols, w),
@@ -704,12 +755,12 @@
         hrR=dma(3, ny),
         brS=dma(ny),
         brR=dma(ny),
-        bzS=dma(ny),
-        bzR=dma(ny),
-        zrS=dma(nz),
-        zrR=dma(nz),
-        bkS=dma(2),
-        bkR=dma(2),
+        bzS=dma(depth - kp + 1, ny),
+        bzR=dma(depth - kp + 1, ny),
+        zrS=dma(depth - kp, nz),
+        zrR=dma(depth - kp, nz),
+        bkS=dma(s),
+        bkR=dma(s),
         pkS=dma(s, NSEP),
         pkR=dma(s, NSEP),
         xS=dma(NSEP),

time: 101 us -> 98.5 us (0.975)
  Pallas kernels: 97.7 us -> 95.4 us
    pallas_call x1, Pallas kernels: 97.7 us -> 95.4 us  [per_device(): pl.pallas_call(functools.partial(kernel, (ny, nz, depth), operands + list...]
where the time goes in v4:
time: 98.5 us; the launch traced here: 98.3 us
  Pallas kernels  95.4 us (97%)
  local copies, waits for them, and re-layouts  2.26 us (2%)
    pallas_call x1, Pallas kernels, per_device(): pl.pallas_call(functools.partial(kernel, (ny, nz, depth), operands + list...  95.4 us
    unnamed x4, local copies, waits for them, and re-layouts  2.26 us

profile of v4, /device:TPU:1, one launch (start us, length us, event | category | flops | bytes accessed | tf_op | source)
XLA Modules:
  0.0 98.3 jit_solution(5512096831417826147)
XLA Ops:
  0.6 95.4 %shard_map.95 = (f32[160,256]{1,0:T(8,128)}, f32[64,256]{1,0:T(8,128)}) custom-call(s32[1,7]{1,0:T(1,128)} %refs_0_.1, f32[160,256]{1,0:T(8,128)} %bitcast.15, f32[160,640]{1,0:T(8,128)} %bitcast.11, f32[160,896]{1,0:T(8,128)} %bitcast.10, s32[1,896]{1,0:T(1,128)} %refs_4_.1, f32[64,256]{1,0:T(8,128)} %bitcast.17, f32[256,256]{1,0:T(8,128)} %bitcast.12, ...), custom_call_target="tpu_custom_call" | custom-call | tf_op jit(solution)/shard_map/pallas_call | solution.py:772
  96.1 0.0 copy-start
  96.1 1.6 %copy.12 = f32[1,160,256]{2,1,0:T(8,128)} copy(f32[1,160,256]{2,1,0:T(8,128)} %bitcast.14) | data formatting | bytes 327680
  97.7 0.0 copy-done
  97.7 0.6 copy.13
Async XLA Ops:
  96.1 1.6 %copy-start = (f32[64,256]{1,0:T(8,128)S(1)}, f32[64,256]{1,0:T(8,128)}, u32[]{:S(2)}) copy-start(f32[64,256]{1,0:T(8,128)} %get-tuple-element.5) | copy-start | bytes 196612

commit v5 on v4

--- a/solution.py
+++ b/solution.py
@@ -12,6 +12,7 @@
 F32 = jnp.float32
 BF16 = jnp.bfloat16
 NSEP = 4
+HALVES = range(2)
 
 
 def split(x):
@@ -113,6 +114,22 @@
 
     own = ds(q, rows)
     mine = ds(q, cols)
+    n = b.S.shape[1]
+    nh = n // 2
+    ch = cols // 2
+
+    def lanes(h):
+        return pl.ds(h * nh, nh)
+
+    def part(h):
+        return pl.ds(h * ch, ch)
+
+    def chunk(h, index):
+        return pl.ds(pl.multiple_of(h * nh + index * ch, 8), ch)
+
+    def in_half(index, h):
+        return lax.div(index, ny // 2) == h
+
     loads = {}
     for i, (name, dst) in enumerate(
         (
@@ -143,23 +160,29 @@
     loads["src"].wait()
     pl.semaphore_wait(barrier, len(greeted))
 
-    def ag(d):
-        return rcopy(b.S.at[own, :], b.S.at[own, :], b.agS.at[d], b.agR.at[d], at_sep(d))
-
-    for d in (2, 1, 3):
-
-        @pl.when(q + d < NSEP)
-        def _():
-            ag(d).start()
-
-        later(functools.partial(ag, d), q + d < NSEP)
+    def ag(h, d):
+        place = b.S.at[own, lanes(h)]
+        return rcopy(place, place, b.agS.at[h, d], b.agR.at[h, d], at_sep(d))
+
+    for h in HALVES:
+        for d in (2, 1, 3):
+
+            @pl.when(q + d < NSEP)
+            def _():
+                ag(h, d).start()
+
+            later(functools.partial(ag, h, d), q + d < NSEP)
 
     def ssx(d):
         to = lax.rem(q + d, NSEP)
         return rcopy(b.sp.at[ds(to, cols), :], b.ssb.at[q], b.ssS.at[d], b.ssR.at[d], at_sep(d))
 
     loads["ssrc"].wait()
-    b.sp[:, :cols] = b.ssrc[...].T
+    turned = b.ssrc[...].T
+    for i in range(NSEP):
+        for h in HALVES:
+            block = turned[h * nh + i * ch : h * nh + (i + 1) * ch]
+            b.sp[i * cols + h * ch : i * cols + (h + 1) * ch, :cols] = block
     b.ssb[q] = b.sp[mine, :]
     for d in range(1, NSEP):
         ssx(d).start()
@@ -295,29 +318,39 @@
         for m in range(2):
             later(functools.partial(fw, m), core0)
 
-    for d in range(1, NSEP):
-
-        @pl.when(q - d >= 0)
-        def _():
-            ag(d).wait_recv()
-
-    loads["inv"].wait()
-    b.yT[...] = mm3(b.inv[...], b.S[...]).T
-
-    def rs(j, d):
+    def rs(h, j, d):
         to = lax.rem(q + d, NSEP)
         return rcopy(
-            b.TT.at[j, ds(to, cols), :], b.rsb.at[j, d], b.rsS.at[j, d], b.rsR.at[j, d], at_sep(d)
+            b.TT.at[j, chunk(h, to), :],
+            b.rsb.at[j, d, part(h)],
+            b.rsS.at[h, j, d],
+            b.rsR.at[h, j, d],
+            at_sep(d),
         )
 
-    yh, yl = split(b.yT[...])
-    for j in range(depth):
-        bh = b.updh[:, j * cap : (j + 1) * cap]
-        bl = b.updl[:, j * cap : (j + 1) * cap]
-        b.TT[j] = mm(yh, bh) + (mm(yl, bh) + mm(yh, bl))
-        for d in (2, 1, 3):
-            rs(j, d).start()
-            later(functools.partial(rs, j, d))
+    loads["inv"].wait()
+    ih, il = split(b.inv[...])
+    b.ih[...] = ih
+    b.il[...] = il
+    for h in HALVES:
+        for d in range(1, NSEP):
+
+            @pl.when(q - d >= 0)
+            def _():
+                ag(h, d).wait_recv()
+
+        sh, sl = split(b.S[:, lanes(h)])
+        ih = b.ih[...]
+        yT = (mm(ih, sh) + (mm(b.il[...], sh) + mm(ih, sl))).T
+        b.yT[lanes(h), :] = yT
+        yh, yl = split(yT)
+        for j in range(depth):
+            bh = b.updh[:, j * cap : (j + 1) * cap]
+            bl = b.updl[:, j * cap : (j + 1) * cap]
+            b.TT[j, lanes(h), :] = mm(yh, bh) + (mm(yl, bh) + mm(yh, bl))
+            for d in (2, 1, 3):
+                rs(h, j, d).start()
+                later(functools.partial(rs, h, j, d))
 
     def yg(m, d):
         dst, src = ((b.MB, b.PM), (b.NB, b.PN))[m]
@@ -352,6 +385,7 @@
             dst[kp:hi, ds(y, mb), :] = src[kp:hi]
 
     gather_high(0)
+    gather_high(1)
     for d in range(1, NSEP):
         ssx(d).wait_recv()
     sT = jnp.concatenate([b.ssb[i][:, :cols] for i in range(NSEP)], axis=1)
@@ -386,25 +420,34 @@
         prepare(k)
 
 
-    def own_part(k):
+    def own_part(h, k):
         for d in range(1, NSEP):
-            rs(k - 1, d).wait_recv()
-        t = (b.TT[k - 1, mine, :] + b.rsb[k - 1, 1]) + (b.rsb[k - 1, 2] + b.rsb[k - 1, 3])
-        part = jnp.where(lam == k, b.sT[...], 0.0) - picked_by(t, b.pick[k - 1], 1)
+            rs(h, k - 1, d).wait_recv()
+        r = part(h)
+        t = (b.TT[k - 1, chunk(h, q), :] + b.rsb[k - 1, 1, r]) + (
+            b.rsb[k - 1, 2, r] + b.rsb[k - 1, 3, r]
+        )
+        mine_k = jnp.where(lam == k, b.sT[r, :], 0.0) - picked_by(t, b.pick[k - 1], 1)
         if 1 < k <= kp:
-            part = part - chain(b.RP[k - 1], b.Th[k - 1], b.Tl[k - 1])
-        b.RP[k] = part
+            mine_k = mine_k - chain(b.RP[k - 1, r], b.Th[k - 1], b.Tl[k - 1])
+        b.RP[k, r] = mine_k
 
     groups = ((2, kp), (kp, depth), (depth, depth + 1))
     sums_on = (core1, core0, core0)
     sends_to_pair = (core0, core1, core1)
 
     def r1():
-        return rcopy(b.RP.at[1], b.R1, b.cxS.at[3], b.cxR.at[3], at_pair)
-
-    def cx(i):
+        return rcopy(b.RP.at[1], b.R1, b.cxS.at[0, 3], b.cxR.at[0, 3], at_pair)
+
+    def cx(h, i):
         lo, hi = groups[i]
-        return rcopy(b.RP.at[lo:hi], b.CX.at[lo:hi], b.cxS.at[i], b.cxR.at[i], at_pair)
+        return rcopy(
+            b.RP.at[lo:hi, part(h)],
+            b.CX.at[lo:hi, part(h)],
+            b.cxS.at[h, i],
+            b.cxR.at[h, i],
+            at_pair,
+        )
 
     def hr(i, d):
         lo, hi = groups[i]
@@ -415,52 +458,55 @@
             dst = b.HH.at[y, lo - kp : hi - kp]
         return rcopy(src, dst, b.hrS.at[i, d], b.hrR.at[i, d], at_y(d))
 
-    def share(i):
+    def share(h, i):
         lo, hi = groups[i]
 
         @when(sends_to_pair[i])
         def _():
-            cx(i).start()
-
-        later(functools.partial(cx, i), sends_to_pair[i])
+            cx(h, i).start()
+
+        later(functools.partial(cx, h, i), sends_to_pair[i])
 
         @when(sums_on[i])
         def _():
-            cx(i).wait_recv()
-            b.H[lo:hi] = b.RP[lo:hi] + b.CX[lo:hi]
+            cx(h, i).wait_recv()
+            r = part(h)
+            b.H[lo:hi, r] = b.RP[lo:hi, r] + b.CX[lo:hi, r]
             for d in range(1, ny):
-                if i == 0:
+                goes = in_half(y_of(d), h)
+
+                @pl.when(jnp.logical_and(goes, even_at(d)) if i else goes)
+                def _():
                     hr(i, d).start()
-                else:
-
-                    @pl.when(even_at(d))
-                    def _():
-                        hr(i, d).start()
-
-            if i == 0:
-                b.HR[y] = b.H[lo:hi, ds(y, rb), :]
 
         if i:
 
-            @when(solver)
+            @when(solver, in_half(y, h))
             def _():
                 b.HH[y, lo - kp : hi - kp] = b.H[lo:hi, ds(lax.div(y, 2), rh), :]
 
+        else:
+
+            @when(core1, in_half(y, h))
+            def _():
+                b.HR[y] = b.H[lo:hi, ds(y, rb), :]
+
+    for i in range(3):
         for d in range(1, ny):
             later(functools.partial(hr, i, d), sums_on[i], *((even_at(d),) if i else ()))
 
-    own_part(1)
-    r1().start()
-    later(r1)
-    for k in range(2, kp):
-        own_part(k)
-    share(0)
-    for k in range(kp, depth):
-        own_part(k)
-    share(1)
-    own_part(depth)
-    share(2)
-    gather_high(1)
+    for h in HALVES:
+        for k in range(1, kp):
+            own_part(h, k)
+        if h == 1:
+            r1().start()
+            later(r1)
+        share(h, 0)
+        for k in range(kp, depth):
+            own_part(h, k)
+        share(h, 1)
+        own_part(h, depth)
+        share(h, 2)
 
     def br(d):
         place = b.RF.at[2:kp, ds(y, rb), :]
@@ -486,9 +532,9 @@
         place = b.RF.at[2:kp]
         return rcopy(place, place, b.bkS.at[0], b.bkR.at[0], at_pair)
 
-    def back_high(k):
-        place = b.X.at[k]
-        return rcopy(place, place, b.bkS.at[k], b.bkR.at[k], at_pair)
+    def back_high(h, k):
+        place = b.X.at[k, part(h)]
+        return rcopy(place, place, b.bhS.at[h, k], b.bhR.at[h, k], at_pair)
 
     @when(core1)
     def _():
@@ -574,42 +620,42 @@
                 bz(k, d).start()
             b.X[k, ds(lax.div(y, 2), rh), :] = b.BZ[k - kp]
 
-    def arrive(k):
+    def arrive(h, k):
         @when(core0)
         def _():
             for d in range(1, ny):
 
-                @pl.when(even_at(d))
+                @when(even_at(d), in_half(y_of(ny - d), h))
                 def _():
                     bz(k, d).wait_recv()
 
-            back_high(k).start()
+            back_high(h, k).start()
 
         @when(core1)
         def _():
-            back_high(k).wait_recv()
+            back_high(h, k).wait_recv()
 
     for k in range(kp, depth + 1):
         for d in range(1, ny):
             later(functools.partial(bz, k, d), solver)
-        later(functools.partial(back_high, k), core0)
-
-    def pk(j, d):
-        place = b.pkb.at[mine, (j - 1) * cap : j * cap]
-        return rcopy(place, place, b.pkS.at[j, d], b.pkR.at[j, d], at_sep(d))
-
-    def send_picked(j):
-        b.pkb[mine, (j - 1) * cap : j * cap] = picked_by(b.X[j], b.pick[j - 1], 0)
-        for d in (2, 1, 3):
-            pk(j, d).start()
-            later(functools.partial(pk, j, d))
-
-    for j in range(depth, 0, -1):
-        if j >= kp:
-            arrive(j)
-        if j <= kp and j > 1:
-            b.X[j - 1] = b.V[j - 1] - chain(b.X[j], b.Mh[j - 1], b.Ml[j - 1])
-        send_picked(j)
+        for h in HALVES:
+            later(functools.partial(back_high, h, k), core0)
+
+    def pk(h, j, d):
+        place = b.pkb.at[chunk(h, q), (j - 1) * cap : j * cap]
+        return rcopy(place, place, b.pkS.at[h, j, d], b.pkR.at[h, j, d], at_sep(d))
+
+    for h in HALVES:
+        r = part(h)
+        for j in range(depth, 0, -1):
+            if j >= kp:
+                arrive(h, j)
+            if j <= kp and j > 1:
+                b.X[j - 1, r] = b.V[j - 1, r] - chain(b.X[j, r], b.Mh[j - 1], b.Ml[j - 1])
+            b.pkb[chunk(h, q), (j - 1) * cap : j * cap] = picked_by(b.X[j, r], b.pick[j - 1], 0)
+            for d in (2, 1, 3):
+                pk(h, j, d).start()
+                later(functools.partial(pk, h, j, d))
 
     def xo(d):
         to = lax.rem(q + d, NSEP)
@@ -626,36 +672,51 @@
         xo(d).start()
         later(functools.partial(xo, d))
 
-    for j in range(depth, 0, -1):
-        for d in range(1, NSEP):
-            pk(j, d).wait_recv()
-    ph, pw = split(b.pkb[...])
-    uh = b.updh[...]
-    wT = b.yT[...] - (mm(ph, uh, 1, 1) + (mm(pw, uh, 1, 1) + mm(ph, b.updl[...], 1, 1)))
-    b.XB[...] = mm3(b.inv[...], wT.T, 0, 0)
-
-    def fin(d):
+    def fin(h, d):
         to = q - d
-        return rcopy(b.XB.at[ds(to, rows), :], b.fb.at[d], b.fS.at[d], b.fR.at[d], (l, to))
-
-    for d in (2, 1, 3):
-
-        @pl.when(q - d >= 0)
-        def _():
-            fin(d).start()
-
-        later(functools.partial(fin, d), q - d >= 0)
+        return rcopy(
+            b.XB.at[ds(to, rows), lanes(h)],
+            b.fb.at[d, :, lanes(h)],
+            b.fS.at[h, d],
+            b.fR.at[h, d],
+            (l, to),
+        )
+
+    def wait_fin(h, d):
+        place = b.fb.at[d, :, lanes(h)]
+        rcopy(place, place, b.fS.at[h, d], b.fR.at[h, d], at_sep(d)).wait_recv()
+
+    for h in HALVES:
+        for j in range(depth, 0, -1):
+            for d in range(1, NSEP):
+                pk(h, j, d).wait_recv()
+        ph, pw = split(b.pkb[lanes(h), :])
+        uh = b.updh[...]
+        wT = b.yT[lanes(h), :] - (mm(ph, uh, 1, 1) + (mm(pw, uh, 1, 1) + mm(ph, b.updl[...], 1, 1)))
+        wh, wl = split(wT.T)
+        ih = b.ih[...]
+        b.XB[:, lanes(h)] = mm(ih, wh, 0, 0) + (mm(b.il[...], wh, 0, 0) + mm(ih, wl, 0, 0))
+        for d in (2, 1, 3):
+
+            @pl.when(q - d >= 0)
+            def _():
+                fin(h, d).start()
+
+            later(functools.partial(fin, h, d), q - d >= 0)
 
     for d in range(1, NSEP):
         xo(d).wait_recv()
-    b.sol[...] = jnp.concatenate([b.xob[i][:, :cols] for i in range(NSEP)], axis=1)
-    b.out[...] = b.XB[own, :]
-    for d in range(1, NSEP):
-
-        @pl.when(q + d < NSEP)
-        def _():
-            rcopy(b.XB.at[own, :], b.fb.at[d], b.fS.at[d], b.fR.at[d], at_sep(d)).wait_recv()
-            b.out[...] += b.fb[d]
+    b.sol[...] = jnp.concatenate(
+        [b.xob[i][:, h * ch : (h + 1) * ch] for h in HALVES for i in range(NSEP)], axis=1
+    )
+    for h in HALVES:
+        b.out[:, lanes(h)] = b.XB[own, lanes(h)]
+        for d in range(1, NSEP):
+
+            @pl.when(q + d < NSEP)
+            def _():
+                wait_fin(h, d)
+                b.out[:, lanes(h)] += b.fb[d, :, lanes(h)]
 
     for copy, conditions in drains:
         if conditions:
@@ -733,8 +794,10 @@
         fb=f(NSEP, rows, n),
         xp=f(n, 128),
         xob=f(NSEP, cols, 128),
-        agS=dma(NSEP),
-        agR=dma(NSEP),
+        ih=h(rows, order),
+        il=h(rows, order),
+        agS=dma(2, NSEP),
+        agR=dma(2, NSEP),
         ssS=dma(NSEP),
         ssR=dma(NSEP),
         moS=dma(2, 8),
@@ -747,10 +810,10 @@
         ygR=dma(2, ny),
         fwS=dma(2),
         fwR=dma(2),
-        rsS=dma(depth, NSEP),
-        rsR=dma(depth, NSEP),
-        cxS=dma(4),
-        cxR=dma(4),
+        rsS=dma(2, depth, NSEP),
+        rsR=dma(2, depth, NSEP),
+        cxS=dma(2, 4),
+        cxR=dma(2, 4),
         hrS=dma(3, ny),
         hrR=dma(3, ny),
         brS=dma(ny),
@@ -759,14 +822,16 @@
         bzR=dma(depth - kp + 1, ny),
         zrS=dma(depth - kp, nz),
         zrR=dma(depth - kp, nz),
-        bkS=dma(s),
-        bkR=dma(s),
-        pkS=dma(s, NSEP),
-        pkR=dma(s, NSEP),
+        bkS=dma(1),
+        bkR=dma(1),
+        bhS=dma(2, s),
+        bhR=dma(2, s),
+        pkS=dma(2, s, NSEP),
+        pkR=dma(2, s, NSEP),
         xS=dma(NSEP),
         xR=dma(NSEP),
-        fS=dma(NSEP),
-        fR=dma(NSEP),
+        fS=dma(2, NSEP),
+        fR=dma(2, NSEP),
     )
     operands = ["counts", "xsrc", "xinv", "xupd", "lists", "xssrc", "xsinv", "xcpl", "out", "sol"]
     out, sol = pl.pallas_call(

time: 98.5 us -> 99.1 us (level)
  no operation moved by 1% of the time
where the time goes in v5:
time: 99.1 us; the launch traced here: 98.3 us
  Pallas kernels  95.4 us (96%)
  local copies, waits for them, and re-layouts  2.26 us (2%)
    pallas_call x1, Pallas kernels, per_device(): pl.pallas_call(functools.partial(kernel, (ny, nz, depth), operands + list...  95.4 us
    unnamed x4, local copies, waits for them, and re-layouts  2.26 us

profile of v5, /device:TPU:1, one launch (start us, length us, event | category | flops | bytes accessed | tf_op | source)
XLA Modules:
  0.0 98.3 jit_solution(4649713041713151377)
XLA Ops:
  0.6 95.4 %shard_map.95 = (f32[160,256]{1,0:T(8,128)}, f32[64,256]{1,0:T(8,128)}) custom-call(s32[1,7]{1,0:T(1,128)} %refs_0_.1, f32[160,256]{1,0:T(8,128)} %bitcast.15, f32[160,640]{1,0:T(8,128)} %bitcast.11, f32[160,896]{1,0:T(8,128)} %bitcast.10, s32[1,896]{1,0:T(1,128)} %refs_4_.1, f32[64,256]{1,0:T(8,128)} %bitcast.17, f32[256,256]{1,0:T(8,128)} %bitcast.12, ...), custom_call_target="tpu_custom_call" | custom-call | tf_op jit(solution)/shard_map/pallas_call | solution.py:837
  96.1 0.0 copy-start
  96.1 1.6 %copy.12 = f32[1,160,256]{2,1,0:T(8,128)} copy(f32[1,160,256]{2,1,0:T(8,128)} %bitcast.14) | data formatting | bytes 327680
  97.7 0.0 copy-done
  97.7 0.6 copy.13
Async XLA Ops:
  96.1 1.6 %copy-start = (f32[64,256]{1,0:T(8,128)S(1)}, f32[64,256]{1,0:T(8,128)}, u32[]{:S(2)}) copy-start(f32[64,256]{1,0:T(8,128)} %get-tuple-element.5) | copy-start | bytes 196612

commit v6 on v5

--- a/solution.py
+++ b/solution.py
@@ -190,38 +190,32 @@
 
     loads["sinv"].wait()
     loads["cpl"].wait()
-    sinv = b.sinv[...]
-    b.Mo[...] = mm3(b.cpl[...], sinv)
-    b.No[...] = mm3(sinv, sinv, 0, 0)
-
     def low_of(k, device, slot, m):
         src, dst = ((b.Mo, b.MB), (b.No, b.NB))[m]
         return rcopy(src, dst.at[k], b.moS.at[m, slot], b.mlR.at[m, k], device)
 
-    def start_both(k, device, slot, *conditions):
-        @when(*conditions)
-        def _():
-            for m in range(2):
+    def send_low(m):
+        targets = [(1, at_pair, 0, (core1,))]
+        for k in range(2, kp):
+            reach = 2 ** (k - 2)
+            offsets = [o for o in range(-reach, reach) if o]
+            for slot, o in enumerate(offsets):
+                targets.append((k, (l + 2 * o, q), slot, (core0, lam == k)))
+        for k, device, slot, conditions in targets:
+
+            @when(*conditions)
+            def _():
                 low_of(k, device, slot, m).start()
 
-        for m in range(2):
             later(functools.partial(low_of, k, device, slot, m), *conditions)
-
-    start_both(1, at_pair, 0, core1)
-    for k in range(2, kp):
-        reach = 2 ** (k - 2)
-        slot = 0
-        for o in range(-reach, reach):
-            if o:
-                start_both(k, (l + 2 * o, q), slot, core0, lam == k)
-                slot += 1
-
-    for k in range(1, kp):
-
-        @when(lam == k)
-        def _():
-            b.MB[k] = b.Mo[...]
-            b.NB[k] = b.No[...]
+        for k in range(1, kp):
+
+            @when(lam == k)
+            def _():
+                if m == 0:
+                    b.MB[k] = b.Mo[...]
+                else:
+                    b.NB[k] = b.No[...]
 
     def sc(m, d):
         src, dst = ((b.Mo, b.PM), (b.No, b.PN))[m]
@@ -234,7 +228,8 @@
         rcopy(dst.at[k], dst.at[k], b.scS.at[m, 0], b.scR.at[m, k], at_pair).wait_recv()
 
     high = jnp.logical_and(core0, jnp.logical_and(lam >= kp, owner))
-    for m in range(2):
+
+    def send_high(m):
         has = (high, lam < depth) if m == 0 else (high,)
 
         @when(*has)
@@ -246,6 +241,14 @@
 
         for d in range(1, ny):
             later(functools.partial(sc, m, d), *has)
+
+    sinv = b.sinv[...]
+    b.Mo[...] = mm3(b.cpl[...], sinv)
+    send_high(0)
+    send_low(0)
+    b.No[...] = mm3(sinv, sinv, 0, 0)
+    send_high(1)
+    send_low(1)
 
     wi = lax.broadcasted_iota(jnp.int32, (w, cap), 0)
     pi = lax.broadcasted_iota(jnp.int32, (w, cap), 1)
@@ -274,7 +277,7 @@
         zd = z_of(d)
         return jnp.logical_and(zd >= base, zd < base + size)
 
-    for m in range(2):
+    def along_z(m):
         top = depth - 1 if m == 0 else depth
 
         @when(core0, y != ny // 2)
@@ -294,29 +297,38 @@
 
             later(functools.partial(zm, m, d), *sends)
 
-    def wait_low(k):
-        for m, dst in enumerate((b.MB, b.NB)):
-            rcopy(dst.at[k], dst.at[k], b.moS.at[m, 0], b.mlR.at[m, k], at_pair).wait_recv()
+    def wait_low(m, k):
+        dst = (b.MB, b.NB)[m]
+        rcopy(dst.at[k], dst.at[k], b.moS.at[m, 0], b.mlR.at[m, k], at_pair).wait_recv()
 
     def fw(m):
         place = (b.MB, b.NB)[m].at[2:kp]
         return rcopy(place, place, b.fwS.at[m], b.fwR.at[m], at_pair)
 
-    for k in range(2, kp):
-
-        @when(core0, lam != k)
-        def _():
-            wait_low(k)
-
-    if kp > 2:
-
+    def pass_low(m):
+        if kp > 2:
+            for k in range(2, kp):
+
+                @when(core0, lam != k)
+                def _():
+                    wait_low(m, k)
+
+            @when(core0)
+            def _():
+                fw(m).start()
+
+            later(functools.partial(fw, m), core0)
+
+    def have_low(m):
         @when(core0)
         def _():
-            for m in range(2):
-                fw(m).start()
-
-        for m in range(2):
-            later(functools.partial(fw, m), core0)
+            wait_low(m, 1)
+
+        if kp > 2:
+
+            @when(core1)
+            def _():
+                fw(m).wait_recv()
 
     def rs(h, j, d):
         to = lax.rem(q + d, NSEP)
@@ -351,6 +363,11 @@
             for d in (2, 1, 3):
                 rs(h, j, d).start()
                 later(functools.partial(rs, h, j, d))
+        if h == 0:
+            along_z(0)
+
+    pass_low(0)
+    along_z(1)
 
     def yg(m, d):
         dst, src = ((b.MB, b.PM), (b.NB, b.PN))[m]
@@ -385,7 +402,6 @@
             dst[kp:hi, ds(y, mb), :] = src[kp:hi]
 
     gather_high(0)
-    gather_high(1)
     for d in range(1, NSEP):
         ssx(d).wait_recv()
     sT = jnp.concatenate([b.ssb[i][:, :cols] for i in range(NSEP)], axis=1)
@@ -405,17 +421,7 @@
         b.Nh[k] = nh
         b.Nl[k] = nl
 
-    @when(core0)
-    def _():
-        wait_low(1)
-
-    if kp > 2:
-
-        @when(core1)
-        def _():
-            for m in range(2):
-                fw(m).wait_recv()
-
+    have_low(0)
     for k in range(1, kp):
         prepare(k)
 
@@ -507,6 +513,9 @@
         share(h, 1)
         own_part(h, depth)
         share(h, 2)
+        if h == 0:
+            gather_high(1)
+    pass_low(1)
 
     def br(d):
         place = b.RF.at[2:kp, ds(y, rb), :]
@@ -584,6 +593,7 @@
         for i in range(1, 2 ** (k - kp)):
             later(functools.partial(zr, k, i), solver)
 
+    have_low(1)
     for k in range(1, kp):
         prepare_n(k)
     r1().wait_recv()

time: 99.1 us -> 93 us (0.938)
  Pallas kernels: 95.4 us -> 89.9 us
    pallas_call x1, Pallas kernels: 95.4 us -> 89.9 us  [per_device(): pl.pallas_call(functools.partial(kernel, (ny, nz, depth), operands + list...]
where the time goes in v6:
time: 93 us; the launch traced here: 92.8 us
  Pallas kernels  89.9 us (97%)
  local copies, waits for them, and re-layouts  2.26 us (2%)
    pallas_call x1, Pallas kernels, per_device(): pl.pallas_call(functools.partial(kernel, (ny, nz, depth), operands + list...  89.9 us
    unnamed x4, local copies, waits for them, and re-layouts  2.26 us

profile of v6, /device:TPU:1, one launch (start us, length us, event | category | flops | bytes accessed | tf_op | source)
XLA Modules:
  0.0 92.8 jit_solution(11010534735593960839)
XLA Ops:
  0.6 89.9 %shard_map.95 = (f32[160,256]{1,0:T(8,128)}, f32[64,256]{1,0:T(8,128)}) custom-call(s32[1,7]{1,0:T(1,128)} %refs_0_.1, f32[160,256]{1,0:T(8,128)} %bitcast.15, f32[160,640]{1,0:T(8,128)} %bitcast.11, f32[160,896]{1,0:T(8,128)} %bitcast.10, s32[1,896]{1,0:T(1,128)} %refs_4_.1, f32[64,256]{1,0:T(8,128)} %bitcast.17, f32[256,256]{1,0:T(8,128)} %bitcast.12, ...), custom_call_target="tpu_custom_call" | custom-call | tf_op jit(solution)/shard_map/pallas_call | solution.py:847
  90.5 0.0 copy-start
  90.5 1.6 %copy.12 = f32[1,160,256]{2,1,0:T(8,128)} copy(f32[1,160,256]{2,1,0:T(8,128)} %bitcast.14) | data formatting | bytes 327680
  92.2 0.0 copy-done
  92.2 0.6 copy.13
Async XLA Ops:
  90.5 1.6 %copy-start = (f32[64,256]{1,0:T(8,128)S(1)}, f32[64,256]{1,0:T(8,128)}, u32[]{:S(2)}) copy-start(f32[64,256]{1,0:T(8,128)} %get-tuple-element.5) | copy-start | bytes 196612

commit v7 on v6

--- a/solution.py
+++ b/solution.py
@@ -330,6 +330,38 @@
             def _():
                 fw(m).wait_recv()
 
+    def yg(m, d):
+        dst, src = ((b.MB, b.PM), (b.NB, b.PN))[m]
+        hi = depth if m == 0 else depth + 1
+        return rcopy(
+            src.at[kp:hi], dst.at[kp:hi, ds(y, mb), :], b.ygS.at[m, d], b.ygR.at[m, d], at_y(d)
+        )
+
+    def gather_high(m):
+        hi = depth if m == 0 else depth + 1
+
+        @when(core0)
+        def _():
+            for k in range(kp + 1, hi):
+
+                @pl.when(plane != k)
+                def _():
+                    wait_zm(m, k)
+
+            for d in range(1, ny):
+
+                @pl.when(even_at(d))
+                def _():
+                    yg(m, d).start()
+
+        for d in range(1, ny):
+            later(functools.partial(yg, m, d), core0, even_at(d))
+
+        @when(solver)
+        def _():
+            dst, src = ((b.MB, b.PM), (b.NB, b.PN))[m]
+            dst[kp:hi, ds(y, mb), :] = src[kp:hi]
+
     def rs(h, j, d):
         to = lax.rem(q + d, NSEP)
         return rcopy(
@@ -344,6 +376,7 @@
     ih, il = split(b.inv[...])
     b.ih[...] = ih
     b.il[...] = il
+    along_z(0)
     for h in HALVES:
         for d in range(1, NSEP):
 
@@ -364,44 +397,11 @@
                 rs(h, j, d).start()
                 later(functools.partial(rs, h, j, d))
         if h == 0:
-            along_z(0)
+            along_z(1)
+            gather_high(0)
 
     pass_low(0)
-    along_z(1)
-
-    def yg(m, d):
-        dst, src = ((b.MB, b.PM), (b.NB, b.PN))[m]
-        hi = depth if m == 0 else depth + 1
-        return rcopy(
-            src.at[kp:hi], dst.at[kp:hi, ds(y, mb), :], b.ygS.at[m, d], b.ygR.at[m, d], at_y(d)
-        )
-
-    def gather_high(m):
-        hi = depth if m == 0 else depth + 1
-
-        @when(core0)
-        def _():
-            for k in range(kp + 1, hi):
-
-                @pl.when(plane != k)
-                def _():
-                    wait_zm(m, k)
-
-            for d in range(1, ny):
-
-                @pl.when(even_at(d))
-                def _():
-                    yg(m, d).start()
-
-        for d in range(1, ny):
-            later(functools.partial(yg, m, d), core0, even_at(d))
-
-        @when(solver)
-        def _():
-            dst, src = ((b.MB, b.PM), (b.NB, b.PN))[m]
-            dst[kp:hi, ds(y, mb), :] = src[kp:hi]
-
-    gather_high(0)
+
     for d in range(1, NSEP):
         ssx(d).wait_recv()
     sT = jnp.concatenate([b.ssb[i][:, :cols] for i in range(NSEP)], axis=1)
@@ -513,7 +513,7 @@
         share(h, 1)
         own_part(h, depth)
         share(h, 2)
-        if h == 0:
+        if h == 1:
             gather_high(1)
     pass_low(1)
 
@@ -592,19 +592,6 @@
     for k in range(kp + 1, depth + 1):
         for i in range(1, 2 ** (k - kp)):
             later(functools.partial(zr, k, i), solver)
-
-    have_low(1)
-    for k in range(1, kp):
-        prepare_n(k)
-    r1().wait_recv()
-    b.RF[1] = b.RP[1] + b.R1[...]
-
-    @when(core0)
-    def _():
-        back_low().wait_recv()
-
-    for k in range(1, kp):
-        b.V[k] = chain(b.RF[k], b.Nh[k], b.Nl[k])
 
     @when(solver)
     def _():
@@ -629,6 +616,19 @@
             for d in range(1, ny):
                 bz(k, d).start()
             b.X[k, ds(lax.div(y, 2), rh), :] = b.BZ[k - kp]
+
+    have_low(1)
+    for k in range(1, kp):
+        prepare_n(k)
+    r1().wait_recv()
+    b.RF[1] = b.RP[1] + b.R1[...]
+
+    @when(core0)
+    def _():
+        back_low().wait_recv()
+
+    for k in range(1, kp):
+        b.V[k] = chain(b.RF[k], b.Nh[k], b.Nl[k])
 
     def arrive(h, k):
         @when(core0)

time: 93 us -> 88.6 us (0.953)
  Pallas kernels: 89.9 us -> 85.5 us
    pallas_call x1, Pallas kernels: 89.9 us -> 85.5 us  [per_device(): pl.pallas_call(functools.partial(kernel, (ny, nz, depth), operands + list...]
where the time goes in v7:
time: 88.6 us; the launch traced here: 88.4 us
  Pallas kernels  85.5 us (97%)
  local copies, waits for them, and re-layouts  2.26 us (3%)
    pallas_call x1, Pallas kernels, per_device(): pl.pallas_call(functools.partial(kernel, (ny, nz, depth), operands + list...  85.5 us
    unnamed x4, local copies, waits for them, and re-layouts  2.26 us

profile of v7, /device:TPU:1, one launch (start us, length us, event | category | flops | bytes accessed | tf_op | source)
XLA Modules:
  0.0 88.4 jit_solution(13714258871270397243)
XLA Ops:
  0.6 85.5 %shard_map.95 = (f32[160,256]{1,0:T(8,128)}, f32[64,256]{1,0:T(8,128)}) custom-call(s32[1,7]{1,0:T(1,128)} %refs_0_.1, f32[160,256]{1,0:T(8,128)} %bitcast.15, f32[160,640]{1,0:T(8,128)} %bitcast.11, f32[160,896]{1,0:T(8,128)} %bitcast.10, s32[1,896]{1,0:T(1,128)} %refs_4_.1, f32[64,256]{1,0:T(8,128)} %bitcast.17, f32[256,256]{1,0:T(8,128)} %bitcast.12, ...), custom_call_target="tpu_custom_call" | custom-call | tf_op jit(solution)/shard_map/pallas_call | solution.py:847
  86.1 0.0 copy-start
  86.1 1.6 %copy.12 = f32[1,160,256]{2,1,0:T(8,128)} copy(f32[1,160,256]{2,1,0:T(8,128)} %bitcast.14) | data formatting | bytes 327680
  87.7 0.0 copy-done
  87.7 0.6 copy.13
Async XLA Ops:
  86.1 1.6 %copy-start = (f32[64,256]{1,0:T(8,128)S(1)}, f32[64,256]{1,0:T(8,128)}, u32[]{:S(2)}) copy-start(f32[64,256]{1,0:T(8,128)} %get-tuple-element.5) | copy-start | bytes 196612

commit v8 on v7

--- a/solution.py
+++ b/solution.py
@@ -106,6 +106,18 @@
 
     drains = []
 
+    def settle():
+        for copy, conditions in drains:
+            if conditions:
+
+                @when(*conditions)
+                def _():
+                    copy().wait_send()
+
+            else:
+                copy().wait_send()
+        drains.clear()
+
     def later(copy, *conditions):
         drains.append((copy, conditions))
 
@@ -348,11 +360,12 @@
                 def _():
                     wait_zm(m, k)
 
-            for d in range(1, ny):
-
-                @pl.when(even_at(d))
-                def _():
-                    yg(m, d).start()
+            for h in HALVES:
+                for d in range(1, ny):
+
+                    @when(even_at(d), in_half(y_of(d), h))
+                    def _():
+                        yg(m, d).start()
 
         for d in range(1, ny):
             later(functools.partial(yg, m, d), core0, even_at(d))
@@ -397,8 +410,9 @@
                 rs(h, j, d).start()
                 later(functools.partial(rs, h, j, d))
         if h == 0:
+            gather_high(0)
+        else:
             along_z(1)
-            gather_high(0)
 
     pass_low(0)
 
@@ -665,7 +679,6 @@
             b.pkb[chunk(h, q), (j - 1) * cap : j * cap] = picked_by(b.X[j, r], b.pick[j - 1], 0)
             for d in (2, 1, 3):
                 pk(h, j, d).start()
-                later(functools.partial(pk, h, j, d))
 
     def xo(d):
         to = lax.rem(q + d, NSEP)
@@ -680,7 +693,13 @@
     b.xob[q] = b.xp[mine, :]
     for d in range(1, NSEP):
         xo(d).start()
+
+    settle()
+    for d in range(1, NSEP):
         later(functools.partial(xo, d))
+        for h in HALVES:
+            for j in range(1, depth + 1):
+                later(functools.partial(pk, h, j, d))
 
     def fin(h, d):
         to = q - d
@@ -712,6 +731,9 @@
             def _():
                 fin(h, d).start()
 
+    settle()
+    for h in HALVES:
+        for d in range(1, NSEP):
             later(functools.partial(fin, h, d), q - d >= 0)
 
     for d in range(1, NSEP):
@@ -728,15 +750,7 @@
                 wait_fin(h, d)
                 b.out[:, lanes(h)] += b.fb[d, :, lanes(h)]
 
-    for copy, conditions in drains:
-        if conditions:
-
-            @when(*conditions)
-            def _():
-                copy().wait_send()
-
-        else:
-            copy().wait_send()
+    settle()
 
 
 def per_device(ny, nz, src, inv, upd, lists, counts, ssrc, sinv, cpl):

time: 88.6 us -> 88.4 us (level)
  no operation moved by 1% of the time
where the time goes in v8:
time: 88.4 us; the launch traced here: 88.2 us
  Pallas kernels  85.3 us (96%)
  local copies, waits for them, and re-layouts  2.26 us (3%)
    pallas_call x1, Pallas kernels, per_device(): pl.pallas_call(functools.partial(kernel, (ny, nz, depth), operands + list...  85.3 us
    unnamed x4, local copies, waits for them, and re-layouts  2.26 us

profile of v8, /device:TPU:1, one launch (start us, length us, event | category | flops | bytes accessed | tf_op | source)
XLA Modules:
  0.0 88.2 jit_solution(7849714034906107004)
XLA Ops:
  0.6 85.3 %shard_map.95 = (f32[160,256]{1,0:T(8,128)}, f32[64,256]{1,0:T(8,128)}) custom-call(s32[1,7]{1,0:T(1,128)} %refs_0_.1, f32[160,256]{1,0:T(8,128)} %bitcast.15, f32[160,640]{1,0:T(8,128)} %bitcast.11, f32[160,896]{1,0:T(8,128)} %bitcast.10, s32[1,896]{1,0:T(1,128)} %refs_4_.1, f32[64,256]{1,0:T(8,128)} %bitcast.17, f32[256,256]{1,0:T(8,128)} %bitcast.12, ...), custom_call_target="tpu_custom_call" | custom-call | tf_op jit(solution)/shard_map/pallas_call | solution.py:861
  85.9 0.0 copy-start
  86.0 1.6 %copy.12 = f32[1,160,256]{2,1,0:T(8,128)} copy(f32[1,160,256]{2,1,0:T(8,128)} %bitcast.14) | data formatting | bytes 327680
  87.6 0.0 copy-done
  87.6 0.6 copy.13
Async XLA Ops:
  85.9 1.6 %copy-start = (f32[64,256]{1,0:T(8,128)S(1)}, f32[64,256]{1,0:T(8,128)}, u32[]{:S(2)}) copy-start(f32[64,256]{1,0:T(8,128)} %get-tuple-element.5) | copy-start | bytes 196612
